TPU v7x, 32 devices: a whole 2x2x4 slice. The times are simulated.
32 devices in a mesh: fsdp: 2 (over y), ctx: 4 (over x, core), tp: 4 (over z).
Axes of the slice: x: 2, y: 2, z: 4, core: 2. Of those that a mesh axis runs over, the one named last changes fastest.
Arguments:
- tokens: bfloat16 [12608, 512], P(('fsdp', 'ctx', 'tp')), may hold values from -6 to 6
- w_qkv: float32 [512, 1536], P(('fsdp', 'ctx', 'tp')), may hold values from -0.375 to 0.375
- w_attend: float32 [512, 512], P(('fsdp', 'ctx', 'tp')), may hold values from -0.75 to 0.75
- w_route: float32 [512, 8], P(('fsdp', 'ctx', 'tp')), may hold values from -0.1875 to 0.1875
- gain_one: float32 [512], P(('fsdp', 'ctx', 'tp')), may hold values from 0.5 to 1.5
- shift_one: float32 [512], P(('fsdp', 'ctx', 'tp')), may hold values from -1 to 1
- gain_two: float32 [512], P(('fsdp', 'ctx', 'tp')), may hold values from 0.5 to 1.5
- shift_two: float32 [512], P(('fsdp', 'ctx', 'tp')), may hold values from -1 to 1
- w_up: float32 [8, 512, 2048], P(None, ('fsdp', 'ctx'), 'tp'), may hold values from -0.25 to 0.25
- w_down: float32 [8, 512, 2048], P(None, ('fsdp', 'ctx'), 'tp'), may hold values from -0.75 to 0.75
- routes: int32 [12608, 2], P(('fsdp', 'ctx')), may hold values from 0 to 7, all different within a row
- priority: int32 [8, 1576], P(('fsdp', 'ctx')), may hold values from 0 to 1575, each once within a row
- cotangent: bfloat16 [12608, 512], P(('fsdp', 'ctx', 'tp')), may hold values from -6 to 6
Outputs:
- output: bfloat16 [12608, 512], P(('fsdp', 'ctx', 'tp'))
- grad_tokens: bfloat16 [12608, 512], P(('fsdp', 'ctx', 'tp'))
- grad_qkv: float32 [512, 1536], P(('fsdp', 'ctx', 'tp'))
- grad_attend: float32 [512, 512], P(('fsdp', 'ctx', 'tp'))
- grad_route: float32 [512, 8], P(('fsdp', 'ctx', 'tp'))
- grad_gain_one: float32 [512], P(('fsdp', 'ctx', 'tp'))
- grad_shift_one: float32 [512], P(('fsdp', 'ctx', 'tp'))
- grad_gain_two: float32 [512], P(('fsdp', 'ctx', 'tp'))
- grad_shift_two: float32 [512], P(('fsdp', 'ctx', 'tp'))
- grad_up: float32 [8, 512, 2048], P(None, ('fsdp', 'ctx'), 'tp')
- grad_down: float32 [8, 512, 2048], P(None, ('fsdp', 'ctx'), 'tp')
Inputs may be any that keep to these rules, and one draw needn't show every extreme that they name: `routes`: each row names 2 different experts, and every expert is named by some row. `priority`: each row is a permutation of 0 to 1575.
All inputs are finite; a program needn't handle non-finite values.
Results may differ from a plain program's by a relative error of at most 0.015.
The roundings to bfloat16 on the way count: a program that leaves them out, or rounds other values in their place, can miss the bound.
Values may be sent and summed in bfloat16 or wider, within the bound.
No kernel may reach another device: no remote copies, remote signals or barrier semaphores. Data moves between devices by JAX's collectives and lax.ppermute only.
A program may use at most 192 MiB of HBM per device.

v0:
```python
from functools import partial
import math

import jax
import jax.numpy as jnp
from jax import lax
from jax.experimental import pallas as pl
from jax.experimental.pallas import tpu as pltpu
from jax.sharding import PartitionSpec as P


D = 512
HEADS = 8
HEAD = 64
SEQ = 197
TOP = 2
EXPERTS = 8

LANES = 128
ROWS = 208
WIDE = 3 * D + D + LANES
SIDE = 4 * D

epsilon = 1e-06
low_type = jnp.bfloat16
full_type = jnp.float32
ALL_AXES = ("fsdp", "ctx", "tp")
ROW_AXES = ("fsdp", "ctx")
VMEM_LIMIT = 58 * 1024 * 1024


def norm_forward(values):
    center = values - jnp.mean(values, axis=-1, keepdims=True)
    spread = jnp.mean(center * center, axis=-1, keepdims=True)
    inv_scale = lax.rsqrt(spread + epsilon)
    return (center * inv_scale, inv_scale)


def norm_backward(grad_norm, normed, inv_scale, gain_row):
    scaled = grad_norm * gain_row
    centred = scaled - jnp.mean(scaled, axis=-1, keepdims=True)
    return inv_scale * (centred - normed * jnp.mean(scaled * normed, axis=-1, keepdims=True))


def mul(left, right):
    return jnp.dot(left, right, preferred_element_type=full_type)


def rows_product(left, right):
    return lax.dot_general(
        left, right, (((0,), (0,)), ((), ())), preferred_element_type=full_type
    )


def times_transpose(left, right):
    return lax.dot_general(
        left, right, (((1,), (1,)), ((), ())), preferred_element_type=full_type
    )


def call(kernel, out_shape, **options):
    return pl.pallas_call(
        kernel,
        out_shape=out_shape,
        compiler_params=pltpu.CompilerParams(vmem_limit_bytes=VMEM_LIMIT),
        **options,
    )


def shape(dims, kind):
    return jax.ShapeDtypeStruct(dims, kind)


def route_kernel(
    capacity, order_row, order_col, routes_row, routes_col, slot_row_ref, slot_col_ref
):
    total = order_row.shape[1]
    first, second = routes_col[:, 0:1], routes_col[:, 1:2]
    lane = lax.broadcasted_iota(jnp.int32, (total, LANES), 1)
    picks_first = (first == lane).astype(full_type)
    picks_second = (second == lane).astype(full_type)
    picks = jnp.concatenate([picks_first, picks_second], axis=1).astype(low_type)
    count_first = jnp.sum(picks_first, axis=0, keepdims=True)
    row = lax.broadcasted_iota(jnp.int32, (EXPERTS, total), 0)
    first_row, second_row = routes_row[0:1, :], routes_row[1:2, :]
    across_first = (first_row == row).astype(full_type)
    across_second = (second_row == row).astype(full_type)
    across = jnp.concatenate([across_first, across_second], axis=0).astype(low_type)
    count_across = jnp.sum(across_first, axis=1, keepdims=True)
    bound = jnp.float32(capacity)
    for start in range(0, total, LANES):
        block = pl.ds(start, LANES)
        earlier = (order_row[...] < order_col[block, :]).astype(full_type).astype(low_type)
        counts = mul(earlier, picks)
        mine, other = routes_col[block, 0:1], routes_col[block, 1:2]
        lane_b = lax.broadcasted_iota(jnp.int32, (LANES, LANES), 1)
        slot = jnp.where(
            mine == lane_b,
            counts[:, :LANES],
            jnp.where(other == lane_b, counts[:, LANES:] + count_first, -1.0),
        )
        slot_col_ref[block, :] = jnp.where(slot < bound, slot, -1.0).astype(jnp.int32)
        counts_t = times_transpose(across, earlier)
        row_b = lax.broadcasted_iota(jnp.int32, (EXPERTS, LANES), 0)
        slot_t = jnp.where(
            routes_row[0:1, block] == row_b,
            counts_t[:EXPERTS, :],
            jnp.where(
                routes_row[1:2, block] == row_b, counts_t[EXPERTS:, :] + count_across, -1.0
            ),
        )
        slot_row_ref[:, block] = jnp.where(slot_t < bound, slot_t, -1.0).astype(jnp.int32)


def dispatch_mask(slot_row, slots):
    total = slot_row.shape[-1]
    return lax.broadcasted_iota(jnp.int32, (slots, total), 0) == slot_row


def combine_mask(slot_col, expert, slots):
    total = slot_col.shape[0]
    lane = lax.broadcasted_iota(jnp.int32, (total, LANES), 1)
    mine = jnp.sum(jnp.where(lane == expert, slot_col, 0), axis=1, keepdims=True)
    return lax.broadcasted_iota(jnp.int32, (total, slots), 1) == mine


def as_low(mask):
    return mask.astype(full_type).astype(low_type)


def join_parts(part_refs, whole):
    own = part_refs[0].shape[0]
    for index, part in enumerate(part_refs):
        whole[index * own : (index + 1) * own, :] = part[...]


def gather_kernel(parts, slot_row_ref, *refs):
    part_refs, (out_ref, whole) = refs[:parts], refs[parts:]

    @pl.when(pl.program_id(0) == 0)
    def _():
        join_parts(part_refs, whole)

    mask = dispatch_mask(slot_row_ref[0], out_ref.shape[1])
    out_ref[0] = mul(as_low(mask), whole[...]).astype(low_type)


def side_rows(pack_ref):
    return jnp.transpose(pack_ref[:, SIDE:].astype(full_type))


def experts_kernel(parts, slot_row_ref, slot_col_ref, cot_ref, up_ref, down_ref, side_ref, *refs):
    part_refs, refs = refs[:parts], refs[parts:]
    (rows_out, weighted_out, grad_pre_out), refs = refs[:3], refs[3:]
    group_outs, (rows_ref, gates, grad_gates, total_acc) = refs[:parts], refs[parts:]
    expert = pl.program_id(0)
    slots = cot_ref.shape[1]

    @pl.when(expert == 0)
    def _():
        join_parts(part_refs, rows_ref)
        route_t = side_rows(side_ref)[:EXPERTS].astype(low_type)
        logits = times_transpose(route_t, rows_ref[...])
        raised = jnp.exp(logits - jnp.max(logits, axis=0, keepdims=True))
        gates[...] = raised / jnp.sum(raised, axis=0, keepdims=True)
        total_acc[...] = jnp.zeros_like(total_acc)

    mask = dispatch_mask(slot_row_ref[0], slots)
    expert_in = mul(as_low(mask), rows_ref[...]).astype(low_type)
    gate_row = gates[pl.ds(expert, 1), :]
    weight = jnp.sum(jnp.where(mask, gate_row, 0.0), axis=1, keepdims=True)
    pre = mul(expert_in, up_ref[0, 0])
    grad_hidden = mul(cot_ref[0], down_ref[0, 0])
    slope = math.sqrt(2.0 / math.pi)
    square = pre * pre
    bent = jnp.tanh(slope * (pre + 0.044715 * (pre * square)))
    half = 0.5 * (1.0 + bent)
    hidden = (pre * half).astype(low_type).astype(full_type)
    pull = half + 0.5 * pre * (1.0 - bent * bent) * (slope * (1.0 + (3 * 0.044715) * square))
    grad_weight = jnp.sum(hidden * grad_hidden, axis=1, keepdims=True)
    grad_gates[pl.ds(expert, 1), :] = jnp.sum(
        jnp.where(mask, grad_weight, 0.0), axis=0, keepdims=True
    )
    grad_pre = (weight * grad_hidden * pull).astype(low_type)
    rows_out[0] = expert_in
    weighted_out[0] = (weight * hidden).astype(low_type)
    grad_pre_out[0] = grad_pre
    grad_in = times_transpose(grad_pre, up_ref[0, 0]).astype(low_type)
    back = as_low(combine_mask(slot_col_ref[...], expert, slots))
    total_acc[...] += mul(back, grad_in)

    @pl.when(expert == EXPERTS - 1)
    def _():
        own = part_refs[0].shape[0]
        total = rows_ref.shape[0]
        for index, out in enumerate(group_outs):
            out[:own, :] = total_acc[index * own : (index + 1) * own, :].astype(low_type)
            gates_part = pltpu.roll(grad_gates[...], (total - index * own) % total, 1)[:, :D]
            high = gates_part.astype(low_type).astype(full_type)
            pair = jnp.concatenate([high, gates_part - high], axis=0)
            out[own:, :] = pair.astype(low_type)


def weights_kernel(rows_ref, cot_ref, weighted_ref, grad_pre_ref, out_ref):
    out_ref[0, 0] = rows_product(rows_ref[0], grad_pre_ref[0]).astype(low_type)
    out_ref[0, 1] = rows_product(cot_ref[0], weighted_ref[0]).astype(low_type)


def combine_kernel(slot_col_ref, weighted_ref, down_ref, *refs):
    outs, total_acc = refs[:-1], refs[-1]
    expert = pl.program_id(0)

    @pl.when(expert == 0)
    def _():
        total_acc[...] = jnp.zeros_like(total_acc)

    expert_out = times_transpose(weighted_ref[0], down_ref[0, 0]).astype(low_type)
    back = as_low(combine_mask(slot_col_ref[...], expert, weighted_ref.shape[1]))
    total_acc[...] += mul(back, expert_out)

    @pl.when(expert == EXPERTS - 1)
    def _():
        own = outs[0].shape[0]
        for index, out in enumerate(outs):
            out[...] = total_acc[index * own : (index + 1) * own, :].astype(low_type)


def head_masks():
    lane = lax.broadcasted_iota(jnp.int32, (1, LANES), 1)
    left = (lane < HEAD).astype(full_type).astype(low_type)
    return (left, 1.0 - left)


def softmax_rows(queries, keys):
    scores = times_transpose(queries, keys) * (1.0 / math.sqrt(HEAD))
    column = lax.broadcasted_iota(jnp.int32, scores.shape, 1)
    scores = jnp.where(column < SEQ, scores, -1e30)
    raised = jnp.exp(scores - jnp.max(scores, axis=-1, keepdims=True))
    return raised / jnp.sum(raised, axis=-1, keepdims=True)


def head_pairs(images):
    for image in range(images):
        rows = pl.ds(image * ROWS, ROWS)
        for pair in range(HEADS * HEAD // LANES):
            yield rows, tuple(
                pl.ds(part * D + pair * LANES, LANES) for part in range(3)
            )


def forward_kernel(places, block, offset_ref, tokens_ref, *refs):
    pieces, (a_two_ref, y_ref, proj_ref, context_ref, pack_ref) = refs[:-5], refs[-5:]
    for piece, place in zip(pieces, places):
        for index, at in enumerate(place):
            start = pl.multiple_of(offset_ref[at], block)
            pack_ref[pl.ds(start, block), :] = piece[index * block : (index + 1) * block, :]
    side = side_rows(pack_ref)
    values = tokens_ref[...].astype(full_type)
    images = tokens_ref.shape[0] // ROWS
    normed, _ = norm_forward(values)
    a_one = (normed * side[8:9] + side[9:10]).astype(low_type)
    proj_ref[...] = mul(a_one, pack_ref[:, : 3 * D]).astype(low_type)
    masks = head_masks()
    lane = lax.broadcasted_iota(jnp.int32, (ROWS, LANES), 1)
    for rows, (q_at, k_at, v_at) in head_pairs(images):
        queries, keys, vals = proj_ref[rows, q_at], proj_ref[rows, k_at], proj_ref[rows, v_at]
        both = [
            mul(softmax_rows(queries * mask, keys).astype(low_type), vals) for mask in masks
        ]
        context_ref[rows, q_at] = jnp.where(lane < HEAD, both[0], both[1]).astype(low_type)
    y_one = values + mul(context_ref[...], pack_ref[:, 3 * D : SIDE])
    y_ref[...] = y_one
    normed_two, _ = norm_forward(y_one)
    a_two_ref[...] = (normed_two * side[10:11] + side[11:12]).astype(low_type)


def backward_kernel(
    parts,
    block,
    offset_ref,
    a_two_ref,
    y_ref,
    cot_ref,
    context_ref,
    proj_ref,
    tokens_ref,
    pack_ref,
    *refs,
):
    grad_refs, grad_tokens_ref, outs = refs[:parts], refs[parts], refs[parts + 1 : -3]
    grad_pack_ref, grad_proj, grad_context = refs[-3:]
    side = side_rows(pack_ref)
    gain_a, offset_a, gain_b = side[8:9], side[9:10], side[10:11]
    route_t = side[:EXPERTS].astype(low_type)
    a_two = a_two_ref[...]
    images = a_two.shape[0] // ROWS
    logits = times_transpose(route_t, a_two)
    raised = jnp.exp(logits - jnp.max(logits, axis=0, keepdims=True))
    gates = raised / jnp.sum(raised, axis=0, keepdims=True)
    own = a_two.shape[0]
    arrived = grad_refs[0][...].astype(full_type)
    for part in grad_refs[1:]:
        arrived += part[...].astype(full_type)
    grad_gates = arrived[own : own + EXPERTS, :own] + arrived[own + EXPERTS :, :own]
    grad_logits = (
        gates * (grad_gates - jnp.sum(gates * grad_gates, axis=0, keepdims=True))
    ).astype(low_type)
    grad_route = mul(grad_logits, a_two)
    grad_a_two = arrived[:own] + rows_product(grad_logits, route_t)
    normed_two, inv_two = norm_forward(y_ref[...])
    grad_gain_b = jnp.sum(grad_a_two * normed_two, axis=0, keepdims=True)
    grad_offset_b = jnp.sum(grad_a_two, axis=0, keepdims=True)
    grad_y = cot_ref[...].astype(full_type) + norm_backward(
        grad_a_two, normed_two, inv_two, gain_b
    )
    grad_branch = grad_y.astype(low_type)
    grad_pack_ref[:, 3 * D : SIDE] = rows_product(context_ref[...], grad_branch).astype(low_type)
    grad_context[...] = times_transpose(grad_branch, pack_ref[:, 3 * D : SIDE]).astype(low_type)
    masks = head_masks()
    scale = 1.0 / math.sqrt(HEAD)
    for rows, (q_at, k_at, v_at) in head_pairs(images):
        queries, keys, vals = proj_ref[rows, q_at], proj_ref[rows, k_at], proj_ref[rows, v_at]
        grads = grad_context[rows, q_at]
        grad_q, grad_k, grad_v = 0.0, 0.0, 0.0
        for mask in masks:
            own_q, own_k, own_g = queries * mask, keys * mask, grads * mask
            probs = softmax_rows(own_q, keys)
            grad_probs = times_transpose(own_g, vals)
            dots = jnp.sum(probs * grad_probs, axis=-1, keepdims=True)
            grad_scores = (probs * (grad_probs - dots)).astype(low_type)
            grad_v += rows_product(probs.astype(low_type), own_g)
            grad_q += mul(grad_scores, own_k)
            grad_k += rows_product(grad_scores, own_q)
        grad_proj[rows, q_at] = (grad_q * scale).astype(low_type)
        grad_proj[rows, k_at] = (grad_k * scale).astype(low_type)
        grad_proj[rows, v_at] = grad_v.astype(low_type)
    values = tokens_ref[...].astype(full_type)
    normed_one, inv_one = norm_forward(values)
    a_one = (normed_one * gain_a + offset_a).astype(low_type)
    grad_pack_ref[:, : 3 * D] = rows_product(a_one, grad_proj[...]).astype(low_type)
    grad_a_one = times_transpose(grad_proj[...], pack_ref[:, : 3 * D])
    grad_gain_a = jnp.sum(grad_a_one * normed_one, axis=0, keepdims=True)
    grad_offset_a = jnp.sum(grad_a_one, axis=0, keepdims=True)
    grad_tokens_ref[...] = (
        grad_y + norm_backward(grad_a_one, normed_one, inv_one, gain_a)
    ).astype(low_type)
    row = lax.broadcasted_iota(jnp.int32, (EXPERTS, D), 0)
    norms = jnp.where(
        row == 0,
        grad_gain_a,
        jnp.where(
            row == 1,
            grad_offset_a,
            jnp.where(row == 2, grad_gain_b, jnp.where(row == 3, grad_offset_b, 0.0)),
        ),
    )
    spare = jnp.zeros((LANES - 2 * EXPERTS, D), full_type)
    sides = jnp.concatenate([grad_route, norms, spare], axis=0)
    grad_pack_ref[:, SIDE:] = jnp.transpose(sides).astype(low_type)
    at = 0
    for out in outs:
        for index in range(out.shape[0] // block):
            start = pl.multiple_of(offset_ref[at], block)
            out[index * block : (index + 1) * block, :] = grad_pack_ref[pl.ds(start, block), :]
            at += 1


def pad_images(rows):
    width = rows.shape[-1]
    images = rows.shape[0] // SEQ
    apart = rows.reshape(images, SEQ, width)
    return jnp.pad(apart, ((0, 0), (0, ROWS - SEQ), (0, 0))).reshape(images * ROWS, width)


def drop_padding(rows):
    width = rows.shape[-1]
    images = rows.shape[0] // ROWS
    return rows.reshape(images, ROWS, width)[:, :SEQ].reshape(images * SEQ, width)


def swap(blocks, axis_name):
    return lax.all_to_all(blocks, axis_name, 0, 0, tiled=True)


def add_up(blocks, axis_name):
    return jnp.sum(swap(blocks, axis_name).astype(full_type), axis=0)


def rotate(value, axis_name, step):
    size = lax.axis_size(axis_name)
    return lax.ppermute(value, axis_name, [(i, (i + step) % size) for i in range(size)])


def cross(value, axis_name, bit):
    size = lax.axis_size(axis_name)
    return lax.ppermute(value, axis_name, [(i, i ^ bit) for i in range(size)])


def collect(part):
    others = range(1, lax.axis_size("tp"))
    return [part] + [rotate(part, "tp", step) for step in others]


def deliver(parts):
    return parts[:1] + [rotate(part, "tp", -step) for step, part in enumerate(parts) if step]


def near_mesh():
    return lax.axis_size("fsdp") == 2 and lax.axis_size("ctx") == 4 and lax.axis_size("tp") == 4


def pack_offsets(block):
    spot = jnp.arange(32, dtype=jnp.int32)
    core, y, x, back = spot // 16, spot // 8 % 2, spot // 4 % 2, spot % 4
    row = (lax.axis_index("fsdp") ^ y) * 4 + (lax.axis_index("ctx") ^ (2 * x + core))
    return ((row * 4 + (lax.axis_index("tp") - back + 4) % 4) * block).astype(jnp.int32)


def gather_near(pack):
    column = jnp.concatenate(collect(pack), axis=0)
    half = column.shape[0] // 2
    over_x = cross(column, "ctx", 2)
    over_y = cross(column, "fsdp", 1)
    low_half = cross(over_y[:half], "ctx", 2)
    high_half = cross(over_x[half:], "fsdp", 1)
    pieces = [column, over_x, over_y, low_half, high_half]
    pieces += [cross(piece, "ctx", 1) for piece in pieces]
    places = [range(0, 4), range(4, 8), range(8, 12), range(12, 14), range(14, 16)]
    places += [[spot + 16 for spot in place] for place in places]
    return pieces, [list(place) for place in places]


def add_low(left, right):
    return (left.astype(full_type) + right.astype(full_type)).astype(low_type)


def reduce_near(own, other):
    rest = (own.shape[0] // 16, own.shape[1])
    sums = add_low(own, cross(other, "ctx", 1)).reshape((2, 2, 4) + rest)
    far = sums[1, 1]
    by_x = cross(far[:2], "ctx", 2)
    by_y = cross(far[2:], "fsdp", 1)
    to_y = jnp.concatenate([add_low(sums[1, 0, :2], by_x), sums[1, 0, 2:]], axis=0)
    to_x = jnp.concatenate([sums[0, 1, :2], add_low(sums[0, 1, 2:], by_y)], axis=0)
    near_x = cross(to_x, "ctx", 2)
    near_y = cross(to_y, "fsdp", 1)
    column = add_low(add_low(sums[0, 0], near_x), near_y)
    arrived = deliver([column[step] for step in range(4)])
    return sum(part.astype(full_type) for part in arrived)


def gather_far(pack):
    wide = lax.all_gather(pack, "tp", axis=0, tiled=True)
    return [lax.all_gather(wide, ROW_AXES, axis=0, tiled=True)], [[0]]


def reduce_far(grad_pack):
    sizes = tuple(lax.axis_size(name) for name in ALL_AXES)
    own = grad_pack.shape[0] // math.prod(sizes)
    rest = (own, grad_pack.shape[1])
    blocks = grad_pack.reshape(sizes + rest)
    blocks = add_up(jnp.moveaxis(blocks, 1, 0), "ctx").astype(low_type)
    blocks = add_up(jnp.moveaxis(blocks, 1, 0), "tp").astype(low_type)
    return add_up(blocks, "fsdp")


def block_step(
    tokens,
    w_qkv,
    w_attend,
    w_route,
    gain_one,
    shift_one,
    gain_two,
    shift_two,
    w_up,
    w_down,
    routes,
    priority,
    cotangent,
):
    tok_rows = tokens.shape[0]
    tp_size = lax.axis_size("tp")
    images = tok_rows // SEQ
    own_rows = images * ROWS
    group_rows = tok_rows * tp_size
    total = own_rows * tp_size
    capacity = group_rows * TOP * 5 // (4 * EXPERTS)
    slots = -(-capacity // 16) * 16
    hidden_width = w_up.shape[2]

    columns = [w_qkv, w_attend, w_route]
    columns += [v[:, None] for v in (gain_one, shift_one, gain_two, shift_two)]
    pack = jnp.concatenate(columns, axis=1).astype(low_type)
    pack = jnp.pad(pack, ((0, 0), (0, WIDE - pack.shape[1])))
    near = near_mesh()
    if near:
        block = pack.shape[0]
        offsets = pack_offsets(block)
        pieces, places = gather_near(pack)
        half = D // 2
        grad_shapes = [shape((half, WIDE), low_type)] * 2
    else:
        block = D
        offsets = jnp.zeros((1,), jnp.int32)
        pieces, places = gather_far(pack)
        grad_shapes = [shape((D, WIDE), low_type)]

    cotangent, w_up, w_down, pieces[0] = lax.optimization_barrier(
        (cotangent, w_up, w_down, pieces[0])
    )
    cot_pad = pad_images(cotangent)
    tok_pad = pad_images(tokens)
    cot_parts = collect(cot_pad)
    both = jnp.stack([w_up, w_down]).astype(low_type)
    both_all = lax.all_gather(both, ROW_AXES, axis=2, tiled=True)

    spread = jnp.pad(
        jnp.concatenate([routes, priority.reshape(-1, 1)], axis=1).reshape(
            group_rows // SEQ, SEQ, TOP + 1
        ),
        ((0, 0), (0, ROWS - SEQ), (0, 0)),
        constant_values=-1,
    ).reshape(tp_size, own_rows, TOP + 1)
    twice = jnp.concatenate([spread[::-1], spread[::-1]], axis=0)
    spread = lax.dynamic_slice_in_dim(twice, tp_size - 1 - lax.axis_index("tp"), tp_size, 0)
    spread = spread.reshape(total, TOP + 1)
    spread_t = spread.T
    slot_row, slot_col = call(
        partial(route_kernel, capacity),
        (shape((EXPERTS, total), jnp.int32), shape((total, LANES), jnp.int32)),
    )(spread_t[TOP:], spread[:, TOP:], spread_t[:TOP], spread[:, :TOP])
    slot_row = slot_row.reshape(EXPERTS, 1, total)

    in_smem = pl.BlockSpec(memory_space=pltpu.SMEM)
    in_vmem = pl.BlockSpec(memory_space=pltpu.VMEM)
    a_two, y_one, proj, context, pack_all = call(
        partial(forward_kernel, places, block),
        (
            shape((own_rows, D), low_type),
            shape((own_rows, D), full_type),
            shape((own_rows, 3 * D), low_type),
            shape((own_rows, D), low_type),
            shape((D, WIDE), low_type),
        ),
        in_specs=[in_smem] + [in_vmem] * (1 + len(pieces)),
    )(offsets, tok_pad, *pieces)

    row_parts = collect(a_two)

    slot_row_spec = pl.BlockSpec((1, 1, total), lambda e: (e, 0, 0))
    slot_col_spec = pl.BlockSpec((total, LANES), lambda e: (0, 0))
    part_spec = pl.BlockSpec((own_rows, D), lambda e: (0, 0))
    grad_spec = pl.BlockSpec((own_rows + 2 * EXPERTS, D), lambda e: (0, 0))
    in_spec = pl.BlockSpec((1, slots, D), lambda e: (e, 0, 0))
    mid_spec = pl.BlockSpec((1, slots, hidden_width), lambda e: (e, 0, 0))
    up_spec = pl.BlockSpec((1, 1, D, hidden_width), lambda e: (0, e, 0, 0))
    down_spec = pl.BlockSpec((1, 1, D, hidden_width), lambda e: (1, e, 0, 0))
    pack_spec = pl.BlockSpec((D, WIDE), lambda e: (0, 0))

    cot_slots = call(
        partial(gather_kernel, tp_size),
        shape((EXPERTS, slots, D), low_type),
        grid=(EXPERTS,),
        in_specs=[slot_row_spec] + [part_spec] * tp_size,
        out_specs=in_spec,
        scratch_shapes=[pltpu.VMEM((total, D), low_type)],
    )(slot_row, *cot_parts)

    expert_in, weighted, grad_pre, *grad_parts = call(
        partial(experts_kernel, tp_size),
        [
            shape((EXPERTS, slots, D), low_type),
            shape((EXPERTS, slots, hidden_width), low_type),
            shape((EXPERTS, slots, hidden_width), low_type),
        ]
        + [shape((own_rows + 2 * EXPERTS, D), low_type)] * tp_size,
        grid=(EXPERTS,),
        in_specs=[slot_row_spec, slot_col_spec, in_spec, up_spec, down_spec, pack_spec]
        + [part_spec] * tp_size,
        out_specs=[in_spec, mid_spec, mid_spec] + [grad_spec] * tp_size,
        scratch_shapes=[
            pltpu.VMEM((total, D), low_type),
            pltpu.VMEM((EXPERTS, total), full_type),
            pltpu.VMEM((EXPERTS, total), full_type),
            pltpu.VMEM((total, D), full_type),
        ],
    )(slot_row, slot_col, cot_slots, both_all, both_all, pack_all, *row_parts)

    grad_arrived = deliver(grad_parts)

    grad_both = call(
        weights_kernel,
        shape((EXPERTS, 2, D, hidden_width), low_type),
        grid=(EXPERTS,),
        in_specs=[in_spec, in_spec, mid_spec, mid_spec],
        out_specs=pl.BlockSpec((1, 2, D, hidden_width), lambda e: (e, 0, 0, 0)),
    )(expert_in, cot_slots, weighted, grad_pre)
    grad_both = lax.psum_scatter(grad_both, ROW_AXES, scatter_dimension=2, tiled=True)

    combined = call(
        combine_kernel,
        [shape((own_rows, D), low_type)] * tp_size,
        grid=(EXPERTS,),
        in_specs=[slot_col_spec, mid_spec, down_spec],
        out_specs=[part_spec] * tp_size,
        scratch_shapes=[pltpu.VMEM((total, D), full_type)],
    )(slot_col, weighted, both_all)

    combined, grad_arrived = lax.optimization_barrier((list(combined), grad_arrived))
    moe_arrived = deliver(combined)

    grad_tokens, *grad_packs = call(
        partial(backward_kernel, tp_size, block),
        [shape((own_rows, D), low_type)] + grad_shapes,
        in_specs=[in_smem] + [in_vmem] * (7 + tp_size),
        scratch_shapes=[
            pltpu.VMEM((D, WIDE), low_type),
            pltpu.VMEM((own_rows, 3 * D), low_type),
            pltpu.VMEM((own_rows, D), low_type),
        ],
    )(offsets, a_two, y_one, cot_pad, context, proj, tok_pad, pack_all, *grad_arrived)

    reduced = reduce_near(*grad_packs) if near else reduce_far(*grad_packs)
    moe_rows = sum(part.astype(full_type) for part in moe_arrived)
    output = drop_padding((y_one + moe_rows).astype(low_type))
    grad_both = grad_both.astype(full_type)
    return (
        output,
        drop_padding(grad_tokens),
        reduced[:, : 3 * D],
        reduced[:, 3 * D : SIDE],
        reduced[:, SIDE : SIDE + EXPERTS],
        reduced[:, SIDE + 8],
        reduced[:, SIDE + 9],
        reduced[:, SIDE + 10],
        reduced[:, SIDE + 11],
        grad_both[:, 0],
        grad_both[:, 1],
    )


def solution(mesh):
    rows = P(ALL_AXES, None)
    vector = P(ALL_AXES)
    weights = P(None, ROW_AXES, "tp")
    group = P(ROW_AXES, None)
    in_specs = (rows,) * 4 + (vector,) * 4 + (weights,) * 2 + (group,) * 2 + (rows,)
    out_specs = (rows,) * 5 + (vector,) * 4 + (weights,) * 2
    return jax.shard_map(
        block_step, mesh=mesh, in_specs=in_specs, out_specs=out_specs, check_vma=False
    )
```

profile of v0, /device:TPU:0, one launch (start us, length us, event | category | flops | bytes accessed | tf_op | source)
XLA Modules:
  0.0 297.6 jit_solution(12618787009204228044)
XLA Ops:
  12.8 5.1 %collective-permute-start.2 = (bf16[16,2176]{1,0:T(8,128)(2,1)S(1)}, bf16[16,2176]{1,0:T(8,128)(2,1)S(1)}, u32[]{:S(2)}, u32[]{:S(2)}) collective-permute-start(bf16[16,2176]{1,0:T(8,128)(2,1)S(1)} %pad.16), channel_id=1, source_target_pairs={{0,3},{1,0},{2,1},{3,2},{4,7},{5,4},{6,5},{7,6},{8,11},{9,8},{10,9... | collective-permute-start | bytes 208904 | tf_op jit(solution)/shard_map/ppermute | solution.py:391
  20.5 4.2 %collective-permute-done.1 = bf16[16,2176]{1,0:T(8,128)(2,1)S(1)} collective-permute-done((bf16[16,2176]{1,0:T(8,128)(2,1)S(1)}, bf16[16,2176]{1,0:T(8,128)(2,1)S(1)}, u32[]{:S(2)}, u32[]{:S(2)}) %collective-permute-start.1) | collective-permute-done | bytes 69664 | tf_op jit(solution)/shard_map/ppermute | solution.py:391
  30.9 1.9 collective-permute-start.14
  32.8 3.4 %collective-permute-done.4.refs_2_ = bf16[64,2176]{1,0:T(8,128)(2,1)S(1)} collective-permute-done((bf16[64,2176]{1,0:T(8,128)(2,1)S(1)}, bf16[64,2176]{1,0:T(8,128)(2,1)S(1)}, u32[]{:S(2)}, u32[]{:S(2)}) %collective-permute-start.4) | collective-permute-done | bytes 278560 | tf_op jit(solution)/shard_map/ppermute | solution.py:396
  39.7 5.5 %collective-permute-done.5.refs_3_ = bf16[32,2176]{1,0:T(8,128)(2,1)S(1)} collective-permute-done((bf16[32,2176]{1,0:T(8,128)(2,1)S(1)}, bf16[32,2176]{1,0:T(8,128)(2,1)S(1)}, u32[]{:S(2)}, u32[]{:S(2)}) %collective-permute-start.5) | collective-permute-done | bytes 139296 | tf_op jit(solution)/shard_map/ppermute | solution.py:396
  45.2 2.8 collective-permute-done.6.refs_4_
  50.9 7.2 %shard_map.212 = (bf16[416,512]{1,0:T(8,128)(2,1)}, f32[416,512]{1,0:T(8,128)}, bf16[416,1536]{1,0:T(8,128)(2,1)}, bf16[416,512]{1,0:T(8,128)(2,1)}, bf16[512,2176]{1,0:T(8,128)(2,1)}) custom-call(s32[32]{0:T(128)} %fusion.19.offset_ref, bf16[416,512]{1,0:T(8,128)(2,1)} %bitcast.76, bf16[64,2176]{1,0:T(8,128)(2,1)} %copy-done.3, bf16[64,2176]{1,0:T(8,128)(2,1)} %copy-done.5, ...), custom_call_target="tpu_custom_call" | custom-call | tf_op jit(solution)/shard_map/pallas_call | solution.py:537
  58.1 3.2 %collective-permute-start.17 = (bf16[416,512]{1,0:T(8,128)(2,1)}, bf16[416,512]{1,0:T(8,128)(2,1)}, u32[]{:S(2)}, u32[]{:S(2)}) collective-permute-start(bf16[416,512]{1,0:T(8,128)(2,1)} %get-tuple-element.52.refs_0_.a_two_ref), channel_id=1, source_target_pairs={{0,3},{1,0},{2,1},{3,2},{4,7},{5,4},{6,5},{7,6},{8,11},{9,8},{10,9... | collective-permute-start | bytes 1277960 | tf_op jit(solution)/shard_map/ppermute | solution.py:391
  66.5 6.2 %shard_map.213 = (s32[8,1664]{1,0:T(8,128)}, s32[1664,128]{1,0:T(8,128)}) custom-call(s32[1,1664]{1,0:T(1,128)} %copy.82.order_row, s32[1664,1]{1,0:T(8,128)} %slice.126.order_col, s32[2,1664]{1,0:T(2,128)} %copy.83.routes_row, s32[1664,2]{1,0:T(8,128)} %bitcast.67), custom_call_target="tpu_custom_call" | custom-call | tf_op jit(solution)/shard_map/pallas_call | solution.py:529
  74.1 5.3 %collective-permute-done.13.refs_2_ = bf16[416,512]{1,0:T(8,128)(2,1)S(1)} collective-permute-done((bf16[416,512]{1,0:T(8,128)(2,1)S(1)}, bf16[416,512]{1,0:T(8,128)(2,1)S(1)}, u32[]{:S(2)}, u32[]{:S(2)}) %collective-permute-start.13) | collective-permute-done | bytes 426016 | tf_op jit(solution)/shard_map/ppermute | solution.py:391
  80.9 11.2 %shard_map.214.cot_ref = bf16[8,496,512]{2,1,0:T(8,128)(2,1)} custom-call(s32[8,1,1664]{2,1,0:T(1,128)} %reshape.77.slot_row_ref, bf16[416,512]{1,0:T(8,128)(2,1)} %bitcast.74, bf16[416,512]{1,0:T(8,128)(2,1)} %copy-done.11, bf16[416,512]{1,0:T(8,128)(2,1)} %copy-done.10, bf16[416,512]{1,0:T(8,128)(2,1)} %copy-done.9), custom_call_target="tpu_custom_call" | custom-call | tf_op jit(solution)/shard_map/pallas_call | solution.py:561
  92.1 23.4 %collective-permute-done.16.refs_2_ = bf16[416,512]{1,0:T(8,128)(2,1)} collective-permute-done((bf16[416,512]{1,0:T(8,128)(2,1)}, bf16[416,512]{1,0:T(8,128)(2,1)}, u32[]{:S(2)}, u32[]{:S(2)}) %collective-permute-start.16) | collective-permute-done | bytes 426016 | tf_op jit(solution)/shard_map/ppermute | solution.py:391
  115.5 36.8 %shard_map.215 = (bf16[8,496,512]{2,1,0:T(8,128)(2,1)}, bf16[8,496,512]{2,1,0:T(8,128)(2,1)}, bf16[8,496,512]{2,1,0:T(8,128)(2,1)}, bf16[432,512]{1,0:T(8,128)(2...) custom-call(s32[8,1,1664]{2,1,0:T(1,128)} %reshape.77.slot_row_ref, ...), custom_call_target="tpu_custom_call" | custom-call | tf_op jit(solution)/shard_map/pallas_call | solution.py:570
  152.3 13.0 %shard_map.218 = bf16[8,2,512,512]{3,2,1,0:T(8,128)(2,1)} custom-call(bf16[8,496,512]{2,1,0:T(8,128)(2,1)} %get-tuple-element.75.rows_ref, bf16[8,496,512]{2,1,0:T(8,128)(2,1)} %shard_map.214.cot_ref, bf16[8,496,512]{2,1,0:T(8,128)(2,1)} %get-tuple-element.53.weighted_ref, bf16[8,496,512]{2,1,0:T(8,128)(2,1)} %get-tuple-element.76.grad_pre_ref), custom_call_target="tpu_custom_call" | custom-call | tf_op jit(solution)/shard_map/pallas_call | solution.py:592
  166.8 1.9 collective-permute-start.20
  168.7 15.2 %shard_map.216 = (bf16[416,512]{1,0:T(8,128)(2,1)}, bf16[416,512]{1,0:T(8,128)(2,1)}, bf16[416,512]{1,0:T(8,128)(2,1)}, bf16[416,512]{1,0:T(8,128)(2,1)}) custom-call(s32[1664,128]{1,0:T(8,128)} %get-tuple-element.46.slot_col_ref, bf16[8,496,512]{2,1,0:T(8,128)(2,1)} %get-tuple-element.53.weighted_ref, ...), custom_call_target="tpu_custom_call" | custom-call | tf_op jit(solution)/shard_map/pallas_call | solution.py:601
  183.9 21.1 %collective-permute-done.19.refs_2_ = bf16[432,512]{1,0:T(8,128)(2,1)S(1)} collective-permute-done((bf16[432,512]{1,0:T(8,128)(2,1)S(1)}, bf16[432,512]{1,0:T(8,128)(2,1)S(1)}, u32[]{:S(2)}, u32[]{:S(2)}) %collective-permute-start.19) | collective-permute-done | bytes 442400 | tf_op jit(solution)/shard_map/ppermute | solution.py:391
  206.0 14.7 %shard_map.217 = (bf16[416,512]{1,0:T(8,128)(2,1)}, bf16[256,2176]{1,0:T(8,128)(2,1)}, bf16[256,2176]{1,0:T(8,128)(2,1)}) custom-call(s32[32]{0:T(128)} %fusion.19.offset_ref, bf16[416,512]{1,0:T(8,128)(2,1)} %get-tuple-element.52.refs_0_.a_two_ref, f32[416,512]{1,0:T(8,128)} %get-tuple-element.45.y_ref, bf16[416,512]{1,0:T(8,128)(2,1)} %bitcast.75, ...), custom_call_target="tpu_custom_call" | custom-call | tf_op jit(solution)/shard_map/pallas_call | solution.py:613
  220.7 3.0 collective-permute-done.24
  227.5 7.1 %collective-permute-done.27 = bf16[2,16,2176]{2,1,0:T(8,128)(2,1)S(1)} collective-permute-done((bf16[2,16,2176]{2,1,0:T(8,128)(2,1)S(1)}, bf16[2,16,2176]{2,1,0:T(8,128)(2,1)S(1)}, u32[]{:S(2)}, u32[]{:S(2)}) %collective-permute-start.27) | collective-permute-done | bytes 139296 | tf_op jit(solution)/shard_map/ppermute | solution.py:396
  239.7 2.7 collective-permute-start.22
  248.6 3.5 %collective-permute-done.21 = bf16[416,512]{1,0:T(8,128)(2,1)S(1)} collective-permute-done((bf16[416,512]{1,0:T(8,128)(2,1)}, bf16[416,512]{1,0:T(8,128)(2,1)S(1)}, u32[]{:S(2)}, u32[]{:S(2)}) %collective-permute-start.21) | collective-permute-done | bytes 426016 | tf_op jit(solution)/shard_map/ppermute | solution.py:391
  252.2 17.3 %collective-permute-start.30 = (bf16[16,2176]{1,0:T(8,128)(2,1)S(1)}, bf16[16,2176]{1,0:T(8,128)(2,1)S(1)}, u32[]{:S(2)}, u32[]{:S(2)}) collective-permute-start(bf16[16,2176]{1,0:T(8,128)(2,1)S(1)} %get-tuple-element.146), channel_id=1, source_target_pairs={{0,2},{1,3},{2,0},{3,1},{4,6},{5,7},{6,4},{7,5},{8,10},{9,11},{10,... | collective-permute-start | bytes 208904 | tf_op jit(solution)/shard_map/ppermute | solution.py:391
  269.5 14.0 %collective-permute-done.22 = bf16[416,512]{1,0:T(8,128)(2,1)S(1)} collective-permute-done((bf16[416,512]{1,0:T(8,128)(2,1)}, bf16[416,512]{1,0:T(8,128)(2,1)S(1)}, u32[]{:S(2)}, u32[]{:S(2)}) %collective-permute-start.22) | collective-permute-done | bytes 426016 | tf_op jit(solution)/shard_map/ppermute | solution.py:391
  (159 shorter events, 53.4 us)
Async XLA Ops:
  7.2 108.3 %all-gather.2.cloned.1.call-start = ((), (), s32[]{:S(2)}) async-start(), calls=%async_computation.1 | async-start | bytes 9437184 | tf_op jit(solution)/shard_map/all_gather | solution.py:516
  27.6 260.1 %reduce-scatter.2.cloned.1.call-start = ((), (), s32[]{:S(2)}) async-start(), calls=%async_computation.2 | async-start | bytes 9437184 | tf_op jit(solution)/shard_map/reduce_scatter | solution.py:599
  29.3 9.4 %collective-permute-start.3 = (bf16[64,2176]{1,0:T(8,128)(2,1)S(1)}, bf16[64,2176]{1,0:T(8,128)(2,1)S(1)}, u32[]{:S(2)}, u32[]{:S(2)}) collective-permute-start(bf16[64,2176]{1,0:T(8,128)(2,1)S(1)} %pad_maximum_fusion.1.refs_0_), channel_id=1, source_target_pairs={{0,8},{4,12},{8,0},{12,4},{1,9},{5,13},{9,1},{13,5},{2,10},{6,14},... | collective-permute-start | bytes 835592 | tf_op jit(solution)/shard_map/ppermute | solution.py:396
  30.9 31.2 %collective-permute-start.14 = (bf16[416,512]{1,0:T(8,128)(2,1)S(1)}, bf16[416,512]{1,0:T(8,128)(2,1)S(1)}, u32[]{:S(2)}, u32[]{:S(2)}) collective-permute-start(bf16[416,512]{1,0:T(8,128)(2,1)S(1)} %bitcast.71), channel_id=1, source_target_pairs={{0,3},{1,0},{2,1},{3,2},{4,7},{5,4},{6,5},{7,6},{8,11},{9,8},{10,9... | collective-permute-start | bytes 1277960 | tf_op jit(solution)/shard_map/ppermute | solution.py:391
  36.3 8.9 %collective-permute-start.5 = (bf16[32,2176]{1,0:T(8,128)(2,1)S(1)}, bf16[32,2176]{1,0:T(8,128)(2,1)S(1)}, u32[]{:S(2)}, u32[]{:S(2)}) collective-permute-start(bf16[32,2176]{1,0:T(8,128)(2,1)S(1)} %slice.123), channel_id=1, source_target_pairs={{0,8},{4,12},{8,0},{12,4},{1,9},{5,13},{9,1},{13,5},{2,10},{6,14},... | collective-permute-start | bytes 417800 | tf_op jit(solution)/shard_map/ppermute | solution.py:396
  37.8 12.3 %collective-permute-start.9 = (bf16[64,2176]{1,0:T(8,128)(2,1)S(1)}, bf16[64,2176]{1,0:T(8,128)(2,1)S(1)}, u32[]{:S(2)}, u32[]{:S(2)}) collective-permute-start(bf16[64,2176]{1,0:T(8,128)(2,1)S(1)} %collective-permute-done.4.refs_2_), channel_id=1, source_target_pairs={{0,4},{4,0},{8,12},{12,8},{1,5},{5,1},{9,13},{13,9},{2,6},{6,2},{1... | collective-permute-start | bytes 835592 | tf_op jit(solution)/shard_map/ppermute | solution.py:396
  38.7 9.3 %collective-permute-start.6 = (bf16[32,2176]{1,0:T(8,128)(2,1)S(1)}, bf16[32,2176]{1,0:T(8,128)(2,1)}, u32[]{:S(2)}, u32[]{:S(2)}) collective-permute-start(bf16[32,2176]{1,0:T(8,128)(2,1)S(1)} %slice.124), channel_id=1, source_target_pairs={{0,16},{16,0},{1,17},{17,1},{2,18},{18,2},{3,19},{19,3},{4,20},{20... | collective-permute-start | bytes 417800 | tf_op jit(solution)/shard_map/ppermute | solution.py:396
  39.5 10.7 %collective-permute-start.8 = (bf16[64,2176]{1,0:T(8,128)(2,1)S(1)}, bf16[64,2176]{1,0:T(8,128)(2,1)}, u32[]{:S(2)}, u32[]{:S(2)}) collective-permute-start(bf16[64,2176]{1,0:T(8,128)(2,1)S(1)} %collective-permute-done.3.refs_1_), channel_id=1, source_target_pairs={{0,4},{4,0},{8,12},{12,8},{1,5},{5,1},{9,13},{13,9},{2,6},{6,2},{1... | collective-permute-start | bytes 835592 | tf_op jit(solution)/shard_map/ppermute | solution.py:396
  49.5 29.9 %collective-permute-start.13 = (bf16[416,512]{1,0:T(8,128)(2,1)S(1)}, bf16[416,512]{1,0:T(8,128)(2,1)S(1)}, u32[]{:S(2)}, u32[]{:S(2)}) collective-permute-start(bf16[416,512]{1,0:T(8,128)(2,1)S(1)} %bitcast.72), channel_id=1, source_target_pairs={{0,2},{1,3},{2,0},{3,1},{4,6},{5,7},{6,4},{7,5},{8,10},{9,11},{10,... | collective-permute-start | bytes 1277960 | tf_op jit(solution)/shard_map/ppermute | solution.py:391
  50.2 29.2 %collective-permute-start.12 = (bf16[416,512]{1,0:T(8,128)(2,1)S(1)}, bf16[416,512]{1,0:T(8,128)(2,1)S(1)}, u32[]{:S(2)}, u32[]{:S(2)}) collective-permute-start(bf16[416,512]{1,0:T(8,128)(2,1)S(1)} %bitcast.73), channel_id=1, source_target_pairs={{0,1},{1,2},{2,3},{3,0},{4,5},{5,6},{6,7},{7,4},{8,9},{9,10},{10,1... | collective-permute-start | bytes 1277960 | tf_op jit(solution)/shard_map/ppermute | solution.py:391
  58.1 34.0 %collective-permute-start.17 = (bf16[416,512]{1,0:T(8,128)(2,1)}, bf16[416,512]{1,0:T(8,128)(2,1)}, u32[]{:S(2)}, u32[]{:S(2)}) collective-permute-start(bf16[416,512]{1,0:T(8,128)(2,1)} %get-tuple-element.52.refs_0_.a_two_ref), channel_id=1, source_target_pairs={{0,3},{1,0},{2,1},{3,2},{4,7},{5,4},{6,5},{7,6},{8,11},{9,8},{10,9... | collective-permute-start | bytes 1277960 | tf_op jit(solution)/shard_map/ppermute | solution.py:391
  61.3 54.2 %collective-permute-start.16 = (bf16[416,512]{1,0:T(8,128)(2,1)}, bf16[416,512]{1,0:T(8,128)(2,1)}, u32[]{:S(2)}, u32[]{:S(2)}) collective-permute-start(bf16[416,512]{1,0:T(8,128)(2,1)} %get-tuple-element.52.refs_0_.a_two_ref), channel_id=1, source_target_pairs={{0,2},{1,3},{2,0},{3,1},{4,6},{5,7},{6,4},{7,5},{8,10},{9,11},{10,... | collective-permute-start | bytes 1277960 | tf_op jit(solution)/shard_map/ppermute | solution.py:391
  62.1 53.4 %collective-permute-start.15 = (bf16[416,512]{1,0:T(8,128)(2,1)}, bf16[416,512]{1,0:T(8,128)(2,1)}, u32[]{:S(2)}, u32[]{:S(2)}) collective-permute-start(bf16[416,512]{1,0:T(8,128)(2,1)} %get-tuple-element.52.refs_0_.a_two_ref), channel_id=1, source_target_pairs={{0,1},{1,2},{2,3},{3,0},{4,5},{5,6},{6,7},{7,4},{8,9},{9,10},{10,1... | collective-permute-start | bytes 1277960 | tf_op jit(solution)/shard_map/ppermute | solution.py:391
  166.4 17.5 %collective-permute-start.18 = (bf16[432,512]{1,0:T(8,128)(2,1)S(1)}, bf16[432,512]{1,0:T(8,128)(2,1)S(1)}, u32[]{:S(2)}, u32[]{:S(2)}) collective-permute-start(bf16[432,512]{1,0:T(8,128)(2,1)S(1)} %copy-done.23), channel_id=1, source_target_pairs={{0,3},{1,0},{2,1},{3,2},{4,7},{5,4},{6,5},{7,6},{8,11},{9,8},{10,9... | collective-permute-start | bytes 1327112 | tf_op jit(solution)/shard_map/ppermute | solution.py:391
  166.5 38.5 %collective-permute-start.19 = (bf16[432,512]{1,0:T(8,128)(2,1)S(1)}, bf16[432,512]{1,0:T(8,128)(2,1)S(1)}, u32[]{:S(2)}, u32[]{:S(2)}) collective-permute-start(bf16[432,512]{1,0:T(8,128)(2,1)S(1)} %copy-done.22), channel_id=1, source_target_pairs={{0,2},{1,3},{2,0},{3,1},{4,6},{5,7},{6,4},{7,5},{8,10},{9,11},{10,... | collective-permute-start | bytes 1327112 | tf_op jit(solution)/shard_map/ppermute | solution.py:391
  166.8 38.3 %collective-permute-start.20 = (bf16[432,512]{1,0:T(8,128)(2,1)S(1)}, bf16[432,512]{1,0:T(8,128)(2,1)S(1)}, u32[]{:S(2)}, u32[]{:S(2)}) collective-permute-start(bf16[432,512]{1,0:T(8,128)(2,1)S(1)} %copy-done.21), channel_id=1, source_target_pairs={{0,1},{1,2},{2,3},{3,0},{4,5},{5,6},{6,7},{7,4},{8,9},{9,10},{10,1... | collective-permute-start | bytes 1327112 | tf_op jit(solution)/shard_map/ppermute | solution.py:391
  225.2 9.4 %collective-permute-start.27 = (bf16[2,16,2176]{2,1,0:T(8,128)(2,1)S(1)}, bf16[2,16,2176]{2,1,0:T(8,128)(2,1)S(1)}, u32[]{:S(2)}, u32[]{:S(2)}) collective-permute-start(bf16[2,16,2176]{2,1,0:T(8,128)(2,1)S(1)} %get-tuple-element.140), channel_id=1, source_target_pairs={{0,8},{4,12},{8,0},{12,4},{1,9},{5,13},{9,1},{13,5},{2,10},{6,14},... | collective-permute-start | bytes 417800 | tf_op jit(solution)/shard_map/ppermute | solution.py:396
  226.7 9.1 %collective-permute-start.25 = (bf16[2,16,2176]{2,1,0:T(8,128)(2,1)S(1)}, bf16[2,16,2176]{2,1,0:T(8,128)(2,1)S(1)}, u32[]{:S(2)}, u32[]{:S(2)}) collective-permute-start(bf16[2,16,2176]{2,1,0:T(8,128)(2,1)S(1)} %get-tuple-element.141), channel_id=1, source_target_pairs={{0,16},{16,0},{1,17},{17,1},{2,18},{18,2},{3,19},{19,3},{4,20},{20... | collective-permute-start | bytes 417800 | tf_op jit(solution)/shard_map/ppermute | solution.py:396
  239.7 12.4 %collective-permute-start.21 = (bf16[416,512]{1,0:T(8,128)(2,1)}, bf16[416,512]{1,0:T(8,128)(2,1)S(1)}, u32[]{:S(2)}, u32[]{:S(2)}) collective-permute-start(bf16[416,512]{1,0:T(8,128)(2,1)} %get-tuple-element.63), channel_id=1, source_target_pairs={{0,3},{1,0},{2,1},{3,2},{4,7},{5,4},{6,5},{7,6},{8,11},{9,8},{10,9... | collective-permute-start | bytes 1277960 | tf_op jit(solution)/shard_map/ppermute | solution.py:391
  239.7 43.8 %collective-permute-start.22 = (bf16[416,512]{1,0:T(8,128)(2,1)}, bf16[416,512]{1,0:T(8,128)(2,1)S(1)}, u32[]{:S(2)}, u32[]{:S(2)}) collective-permute-start(bf16[416,512]{1,0:T(8,128)(2,1)} %get-tuple-element.64), channel_id=1, source_target_pairs={{0,2},{1,3},{2,0},{3,1},{4,6},{5,7},{6,4},{7,5},{8,10},{9,11},{10,... | collective-permute-start | bytes 1277960 | tf_op jit(solution)/shard_map/ppermute | solution.py:391
  242.5 41.1 %collective-permute-start.23 = (bf16[416,512]{1,0:T(8,128)(2,1)}, bf16[416,512]{1,0:T(8,128)(2,1)S(1)}, u32[]{:S(2)}, u32[]{:S(2)}) collective-permute-start(bf16[416,512]{1,0:T(8,128)(2,1)} %get-tuple-element.65), channel_id=1, source_target_pairs={{0,1},{1,2},{2,3},{3,0},{4,5},{5,6},{6,7},{7,4},{8,9},{9,10},{10,1... | collective-permute-start | bytes 1277960 | tf_op jit(solution)/shard_map/ppermute | solution.py:391
  246.6 38.2 %collective-permute-start.29 = (bf16[16,2176]{1,0:T(8,128)(2,1)S(1)}, bf16[16,2176]{1,0:T(8,128)(2,1)S(1)}, u32[]{:S(2)}, u32[]{:S(2)}) collective-permute-start(bf16[16,2176]{1,0:T(8,128)(2,1)S(1)} %get-tuple-element.144), channel_id=1, source_target_pairs={{0,3},{1,0},{2,1},{3,2},{4,7},{5,4},{6,5},{7,6},{8,11},{9,8},{10,9... | collective-permute-start | bytes 208904 | tf_op jit(solution)/shard_map/ppermute | solution.py:391
  247.5 37.3 %collective-permute-start.31 = (bf16[16,2176]{1,0:T(8,128)(2,1)S(1)}, bf16[16,2176]{1,0:T(8,128)(2,1)S(1)}, u32[]{:S(2)}, u32[]{:S(2)}) collective-permute-start(bf16[16,2176]{1,0:T(8,128)(2,1)S(1)} %get-tuple-element.145), channel_id=1, source_target_pairs={{0,1},{1,2},{2,3},{3,0},{4,5},{5,6},{6,7},{7,4},{8,9},{9,10},{10,1... | collective-permute-start | bytes 208904 | tf_op jit(solution)/shard_map/ppermute | solution.py:391
  252.2 32.9 %collective-permute-start.30 = (bf16[16,2176]{1,0:T(8,128)(2,1)S(1)}, bf16[16,2176]{1,0:T(8,128)(2,1)S(1)}, u32[]{:S(2)}, u32[]{:S(2)}) collective-permute-start(bf16[16,2176]{1,0:T(8,128)(2,1)S(1)} %get-tuple-element.146), channel_id=1, source_target_pairs={{0,2},{1,3},{2,0},{3,1},{4,6},{5,7},{6,4},{7,5},{8,10},{9,11},{10,... | collective-permute-start | bytes 208904 | tf_op jit(solution)/shard_map/ppermute | solution.py:391
  (34 other events, 335.3 us)
Sparse Core Ops, SparseCore 0:
  27.8 56.2 all-gather.1
  165.5 71.9 reduce-scatter.1
where the time goes:
time: 298 us
  Pallas kernels  104 us (35%)
  waiting for transfers between devices  98.5 us (33%)
  starting transfers between devices  49.3 us (17%)
  local copies, waits for them, and re-layouts  17.4 us (6%)
  between operations  14.4 us (5%)
  other arithmetic  13.7 us (5%)
    ppermute x18, waiting for transfers between devices, rotate(): lax.ppermute(value, axis_name, [(i, (i + step) % size) for i in range(siz...  73.4 us
    ppermute x18, starting transfers between devices, rotate(): lax.ppermute(value, axis_name, [(i, (i + step) % size) for i in range(siz...  39.1 us
    pallas_call x1, Pallas kernels, block_step(): call(partial(experts_kernel, tp_size), [shape((EXPERTS, slots, D), low_ty...  36.8 us
    ppermute x14, waiting for transfers between devices, cross(): return lax.ppermute(value, axis_name, [(i, i ^ bit) for i in range(size)])  25.1 us
    pallas_call x1, Pallas kernels, block_step(): call(combine_kernel, [shape((own_rows, D), low_type)] * tp_size, grid=(EX...  15.2 us
    pallas_call x1, Pallas kernels, block_step(): call(partial(backward_kernel, tp_size, block), [shape((own_rows, D), low_...  14.7 us
    pallas_call x1, Pallas kernels, block_step(): call(weights_kernel, shape((EXPERTS, 2, D, hidden_width), low_type), grid...  13 us
    pallas_call x1, Pallas kernels, block_step(): call(partial(gather_kernel, tp_size), shape((EXPERTS, slots, D), low_type...  11.2 us
  transfers between devices with their start and end apart: 34, of which 16 were waited for; matrix products, arithmetic and copies ran while one was open for 5% of the time, Pallas kernels for 18%

commit v1 on v0

--- a/solution.py
+++ b/solution.py
@@ -149,24 +149,66 @@
     return jnp.transpose(pack_ref[:, SIDE:].astype(full_type))
 
 
-def experts_kernel(parts, slot_row_ref, slot_col_ref, cot_ref, up_ref, down_ref, side_ref, *refs):
-    part_refs, refs = refs[:parts], refs[parts:]
-    (rows_out, weighted_out, grad_pre_out), refs = refs[:3], refs[3:]
-    group_outs, (rows_ref, gates, grad_gates, total_acc) = refs[:parts], refs[parts:]
+def gates_of(route_t, rows):
+    logits = times_transpose(route_t, rows)
+    raised = jnp.exp(logits - jnp.max(logits, axis=0, keepdims=True))
+    return raised / jnp.sum(raised, axis=0, keepdims=True)
+
+
+def early_kernel(parts, slot_row_ref, side_ref, *refs):
+    part_refs, (out_ref, gates_ref, whole) = refs[:parts], refs[parts:]
+
+    @pl.when(pl.program_id(0) == 0)
+    def _():
+        filled = parts * part_refs[0].shape[0]
+        join_parts(part_refs, whole)
+        whole[filled:, :] = jnp.zeros((whole.shape[0] - filled, D), low_type)
+        gates_ref[...] = gates_of(side_rows(side_ref)[:EXPERTS].astype(low_type), whole[...])
+
+    mask = dispatch_mask(slot_row_ref[0][:, : whole.shape[0]], out_ref.shape[1])
+    out_ref[0] = mul(as_low(mask), whole[...]).astype(low_type)
+
+
+def experts_kernel(
+    slot_row_ref,
+    cot_ref,
+    up_ref,
+    down_ref,
+    side_ref,
+    early_ref,
+    early_gates,
+    last_ref,
+    rows_out,
+    weighted_out,
+    grad_pre_out,
+    grad_in_out,
+    grad_gates_out,
+    rows_ref,
+    gates,
+):
     expert = pl.program_id(0)
     slots = cot_ref.shape[1]
+    total = slot_row_ref.shape[2]
+    tail = rows_ref.shape[0]
+    base = total - tail
 
     @pl.when(expert == 0)
     def _():
-        join_parts(part_refs, rows_ref)
-        route_t = side_rows(side_ref)[:EXPERTS].astype(low_type)
-        logits = times_transpose(route_t, rows_ref[...])
-        raised = jnp.exp(logits - jnp.max(logits, axis=0, keepdims=True))
-        gates[...] = raised / jnp.sum(raised, axis=0, keepdims=True)
-        total_acc[...] = jnp.zeros_like(total_acc)
+        own = last_ref.shape[0]
+        overlap = early_gates.shape[1] - base
+        rows_ref[: tail - own, :] = jnp.zeros((tail - own, D), low_type)
+        rows_ref[tail - own :, :] = last_ref[...]
+        late = gates_of(side_rows(side_ref)[:EXPERTS].astype(low_type), rows_ref[...])
+        gates[:, :base] = early_gates[:, :base]
+        if overlap:
+            lane = lax.broadcasted_iota(jnp.int32, (EXPERTS, overlap), 1)
+            gates[:, base : base + overlap] = jnp.where(
+                lane < tail - own, early_gates[:, base:], late[:, :overlap]
+            )
+        gates[:, base + overlap :] = late[:, overlap:]
 
     mask = dispatch_mask(slot_row_ref[0], slots)
-    expert_in = mul(as_low(mask), rows_ref[...]).astype(low_type)
+    expert_in = early_ref[0] + mul(as_low(mask[:, base:]), rows_ref[...]).astype(low_type)
     gate_row = gates[pl.ds(expert, 1), :]
     weight = jnp.sum(jnp.where(mask, gate_row, 0.0), axis=1, keepdims=True)
     pre = mul(expert_in, up_ref[0, 0])
@@ -178,24 +220,38 @@
     hidden = (pre * half).astype(low_type).astype(full_type)
     pull = half + 0.5 * pre * (1.0 - bent * bent) * (slope * (1.0 + (3 * 0.044715) * square))
     grad_weight = jnp.sum(hidden * grad_hidden, axis=1, keepdims=True)
-    grad_gates[pl.ds(expert, 1), :] = jnp.sum(
+    grad_gates_out[pl.ds(expert, 1), :] = jnp.sum(
         jnp.where(mask, grad_weight, 0.0), axis=0, keepdims=True
     )
     grad_pre = (weight * grad_hidden * pull).astype(low_type)
     rows_out[0] = expert_in
     weighted_out[0] = (weight * hidden).astype(low_type)
     grad_pre_out[0] = grad_pre
-    grad_in = times_transpose(grad_pre, up_ref[0, 0]).astype(low_type)
-    back = as_low(combine_mask(slot_col_ref[...], expert, slots))
-    total_acc[...] += mul(back, grad_in)
+    grad_in_out[0] = times_transpose(grad_pre, up_ref[0, 0]).astype(low_type)
+
+
+def back_kernel(blocks, slot_col_ref, grad_in_ref, grad_gates_ref, *refs):
+    outs, total_acc = refs[:-1], refs[-1]
+    expert = pl.program_id(0)
+    own = total_acc.shape[0] // len(blocks)
+    total = slot_col_ref.shape[0]
+
+    @pl.when(expert == 0)
+    def _():
+        total_acc[...] = jnp.zeros_like(total_acc)
+
+    for index, at in enumerate(blocks):
+        rows = slice(index * own, (index + 1) * own)
+        slot_col = slot_col_ref[at * own : (at + 1) * own, :]
+        back = as_low(combine_mask(slot_col, expert, grad_in_ref.shape[1]))
+        total_acc[rows, :] += mul(back, grad_in_ref[0])
 
     @pl.when(expert == EXPERTS - 1)
     def _():
-        own = part_refs[0].shape[0]
-        total = rows_ref.shape[0]
-        for index, out in enumerate(group_outs):
+        for index, (at, out) in enumerate(zip(blocks, outs)):
             out[:own, :] = total_acc[index * own : (index + 1) * own, :].astype(low_type)
-            gates_part = pltpu.roll(grad_gates[...], (total - index * own) % total, 1)[:, :D]
+            shift = (total - at * own) % total
+            gates_part = pltpu.roll(grad_gates_ref[...], shift, 1)[:, :D]
             high = gates_part.astype(low_type).astype(full_type)
             pair = jnp.concatenate([high, gates_part - high], axis=0)
             out[own:, :] = pair.astype(low_type)
@@ -396,13 +452,18 @@
     return lax.ppermute(value, axis_name, [(i, i ^ bit) for i in range(size)])
 
 
+def steps():
+    size = lax.axis_size("tp")
+    nearest = [step for apart in range(1, size) for step in (apart, size - apart)]
+    return list(dict.fromkeys([0] + nearest))
+
+
 def collect(part):
-    others = range(1, lax.axis_size("tp"))
-    return [part] + [rotate(part, "tp", step) for step in others]
+    return [rotate(part, "tp", step) if step else part for step in steps()]
 
 
 def deliver(parts):
-    return parts[:1] + [rotate(part, "tp", -step) for step, part in enumerate(parts) if step]
+    return [rotate(part, "tp", -step) if step else part for step, part in zip(steps(), parts)]
 
 
 def near_mesh():
@@ -417,7 +478,8 @@
 
 
 def gather_near(pack):
-    column = jnp.concatenate(collect(pack), axis=0)
+    arrived = dict(zip(steps(), collect(pack)))
+    column = jnp.concatenate([arrived[step] for step in range(4)], axis=0)
     half = column.shape[0] // 2
     over_x = cross(column, "ctx", 2)
     over_y = cross(column, "fsdp", 1)
@@ -445,7 +507,7 @@
     near_x = cross(to_x, "ctx", 2)
     near_y = cross(to_y, "fsdp", 1)
     column = add_low(add_low(sums[0, 0], near_x), near_y)
-    arrived = deliver([column[step] for step in range(4)])
+    arrived = deliver([column[step] for step in steps()])
     return sum(part.astype(full_type) for part in arrived)
 
 
@@ -506,13 +568,11 @@
         pieces, places = gather_far(pack)
         grad_shapes = [shape((D, WIDE), low_type)]
 
-    cotangent, w_up, w_down, pieces[0] = lax.optimization_barrier(
-        (cotangent, w_up, w_down, pieces[0])
-    )
     cot_pad = pad_images(cotangent)
     tok_pad = pad_images(tokens)
+    both = jnp.stack([w_up, w_down]).astype(low_type)
+    cot_pad, both, pieces[0] = lax.optimization_barrier((cot_pad, both, pieces[0]))
     cot_parts = collect(cot_pad)
-    both = jnp.stack([w_up, w_down]).astype(low_type)
     both_all = lax.all_gather(both, ROW_AXES, axis=2, tiled=True)
 
     spread = jnp.pad(
@@ -524,7 +584,7 @@
     ).reshape(tp_size, own_rows, TOP + 1)
     twice = jnp.concatenate([spread[::-1], spread[::-1]], axis=0)
     spread = lax.dynamic_slice_in_dim(twice, tp_size - 1 - lax.axis_index("tp"), tp_size, 0)
-    spread = spread.reshape(total, TOP + 1)
+    spread = jnp.concatenate([spread[step] for step in steps()], axis=0)
     spread_t = spread.T
     slot_row, slot_col = call(
         partial(route_kernel, capacity),
@@ -567,26 +627,62 @@
         scratch_shapes=[pltpu.VMEM((total, D), low_type)],
     )(slot_row, *cot_parts)
 
-    expert_in, weighted, grad_pre, *grad_parts = call(
-        partial(experts_kernel, tp_size),
+    early = tp_size - 1
+    early_lanes = -(-early * own_rows // LANES) * LANES
+    late_lanes = total - early * own_rows // LANES * LANES
+    early_gates_spec = pl.BlockSpec((EXPERTS, early_lanes), lambda e: (0, 0))
+    gates_spec = pl.BlockSpec((EXPERTS, total), lambda e: (0, 0))
+    early_in, early_gates = call(
+        partial(early_kernel, early),
+        [
+            shape((EXPERTS, slots, D), low_type),
+            shape((EXPERTS, early_lanes), full_type),
+        ],
+        grid=(EXPERTS,),
+        in_specs=[slot_row_spec, pack_spec] + [part_spec] * early,
+        out_specs=[in_spec, early_gates_spec],
+        scratch_shapes=[pltpu.VMEM((early_lanes, D), low_type)],
+    )(slot_row, pack_all, *row_parts[:early])
+
+    expert_in, weighted, grad_pre, grad_in, grad_gates = call(
+        experts_kernel,
         [
             shape((EXPERTS, slots, D), low_type),
             shape((EXPERTS, slots, hidden_width), low_type),
             shape((EXPERTS, slots, hidden_width), low_type),
-        ]
-        + [shape((own_rows + 2 * EXPERTS, D), low_type)] * tp_size,
+            shape((EXPERTS, slots, D), low_type),
+            shape((EXPERTS, total), full_type),
+        ],
         grid=(EXPERTS,),
-        in_specs=[slot_row_spec, slot_col_spec, in_spec, up_spec, down_spec, pack_spec]
-        + [part_spec] * tp_size,
-        out_specs=[in_spec, mid_spec, mid_spec] + [grad_spec] * tp_size,
+        in_specs=[
+            slot_row_spec,
+            in_spec,
+            up_spec,
+            down_spec,
+            pack_spec,
+            in_spec,
+            early_gates_spec,
+            part_spec,
+        ],
+        out_specs=[in_spec, mid_spec, mid_spec, in_spec, gates_spec],
         scratch_shapes=[
-            pltpu.VMEM((total, D), low_type),
+            pltpu.VMEM((late_lanes, D), low_type),
             pltpu.VMEM((EXPERTS, total), full_type),
-            pltpu.VMEM((EXPERTS, total), full_type),
-            pltpu.VMEM((total, D), full_type),
         ],
-    )(slot_row, slot_col, cot_slots, both_all, both_all, pack_all, *row_parts)
-
+    )(slot_row, cot_slots, both_all, both_all, pack_all, early_in, early_gates, row_parts[-1])
+
+    def back(blocks):
+        return call(
+            partial(back_kernel, blocks),
+            [shape((own_rows + 2 * EXPERTS, D), low_type)] * len(blocks),
+            grid=(EXPERTS,),
+            in_specs=[slot_col_spec, in_spec, gates_spec],
+            out_specs=[grad_spec] * len(blocks),
+            scratch_shapes=[pltpu.VMEM((len(blocks) * own_rows, D), full_type)],
+        )(slot_col, grad_in, grad_gates)
+
+    grad_parts = back((0,)) + back(tuple(range(1, early)))
+    grad_parts += back((early,))
     grad_arrived = deliver(grad_parts)
 
     grad_both = call(

time: 298 us -> 301 us (1.010)
  waiting for transfers between devices: 98.5 us -> 71.5 us
  Pallas kernels: 104 us -> 126 us
  starting transfers between devices: 49.3 us -> 57 us
    ppermute x18, waiting for transfers between devices: 73.4 us -> 48.4 us  [rotate(): lax.ppermute(value, axis_name, [(i, (i + step) % size) for i in range(siz...]
    pallas_call x1 -> x5, Pallas kernels: 36.8 us -> 57.3 us  [the longest x3 24.8 us: back(): call(partial(back_kernel, blocks), [shape((own_rows + 2 * EXPERTS, D), lo...]
    ppermute x18, starting transfers between devices: 39.1 us -> 47.4 us  [rotate(): lax.ppermute(value, axis_name, [(i, (i + step) % size) for i in range(siz...]
    unnamed x49 -> x57, local copies, waits for them, and re-layouts: 4.96 us -> 7.64 us
  transfers between devices with their start and end apart: 34 -> 34, of which waited for: 16 -> 15; matrix products, arithmetic and copies ran while one was open for 5% -> 6% of each run, Pallas kernels for 18% -> 30%
where the time goes in v1:
time: 301 us; the launch traced here: 300 us
  Pallas kernels  126 us (42%)
  waiting for transfers between devices  71.5 us (24%)
  starting transfers between devices  57 us (19%)
  local copies, waits for them, and re-layouts  18.8 us (6%)
  between operations  14.5 us (5%)
  other arithmetic  12.2 us (4%)
    ppermute x18, waiting for transfers between devices, rotate(): lax.ppermute(value, axis_name, [(i, (i + step) % size) for i in range(siz...  48.4 us
    ppermute x18, starting transfers between devices, rotate(): lax.ppermute(value, axis_name, [(i, (i + step) % size) for i in range(siz...  47.4 us
    pallas_call x3, Pallas kernels, back(): call(partial(back_kernel, blocks), [shape((own_rows + 2 * EXPERTS, D), lo...  24.8 us
    ppermute x14, waiting for transfers between devices, cross(): return lax.ppermute(value, axis_name, [(i, i ^ bit) for i in range(size)])  23 us
    pallas_call x1, Pallas kernels, block_step(): call(experts_kernel, [shape((EXPERTS, slots, D), low_type), shape((EXPERT...  22.4 us
    pallas_call x1, Pallas kernels, block_step(): call(combine_kernel, [shape((own_rows, D), low_type)] * tp_size, grid=(EX...  15.2 us
    pallas_call x1, Pallas kernels, block_step(): call(partial(backward_kernel, tp_size, block), [shape((own_rows, D), low_...  14.7 us
    pallas_call x1, Pallas kernels, block_step(): call(weights_kernel, shape((EXPERTS, 2, D, hidden_width), low_type), grid...  13 us
  transfers between devices with their start and end apart: 34, of which 15 were waited for; matrix products, arithmetic and copies ran while one was open for 6% of the time, Pallas kernels for 30%

profile of v1, /device:TPU:0, one launch (start us, length us, event | category | flops | bytes accessed | tf_op | source)
XLA Modules:
  0.0 299.7 jit_solution(17738367094593749046)
XLA Ops:
  12.9 5.1 %collective-permute-start.2 = (bf16[16,2176]{1,0:T(8,128)(2,1)S(1)}, bf16[16,2176]{1,0:T(8,128)(2,1)S(1)}, u32[]{:S(2)}, u32[]{:S(2)}) collective-permute-start(bf16[16,2176]{1,0:T(8,128)(2,1)S(1)} %pad.17), channel_id=1, source_target_pairs={{0,3},{1,0},{2,1},{3,2},{4,7},{5,4},{6,5},{7,6},{8,11},{9,8},{10,9... | collective-permute-start | bytes 208904 | tf_op jit(solution)/shard_map/ppermute | solution.py:447
  21.5 3.4 %collective-permute-done.1 = bf16[16,2176]{1,0:T(8,128)(2,1)S(1)} collective-permute-done((bf16[16,2176]{1,0:T(8,128)(2,1)S(1)}, bf16[16,2176]{1,0:T(8,128)(2,1)S(1)}, u32[]{:S(2)}, u32[]{:S(2)}) %collective-permute-start.1) | collective-permute-done | bytes 69664 | tf_op jit(solution)/shard_map/ppermute | solution.py:447
  28.3 5.3 %collective-permute-done.4.refs_2_ = bf16[64,2176]{1,0:T(8,128)(2,1)S(1)} collective-permute-done((bf16[64,2176]{1,0:T(8,128)(2,1)S(1)}, bf16[64,2176]{1,0:T(8,128)(2,1)S(1)}, u32[]{:S(2)}, u32[]{:S(2)}) %collective-permute-start.4) | collective-permute-done | bytes 278560 | tf_op jit(solution)/shard_map/ppermute | solution.py:452
  38.9 3.6 %collective-permute-done.5.refs_3_ = bf16[32,2176]{1,0:T(8,128)(2,1)S(1)} collective-permute-done((bf16[32,2176]{1,0:T(8,128)(2,1)S(1)}, bf16[32,2176]{1,0:T(8,128)(2,1)S(1)}, u32[]{:S(2)}, u32[]{:S(2)}) %collective-permute-start.5) | collective-permute-done | bytes 139296 | tf_op jit(solution)/shard_map/ppermute | solution.py:452
  48.3 7.8 %shard_map.212 = (bf16[416,512]{1,0:T(8,128)(2,1)}, f32[416,512]{1,0:T(8,128)}, bf16[416,1536]{1,0:T(8,128)(2,1)}, bf16[416,512]{1,0:T(8,128)(2,1)}, bf16[512,2176]{1,0:T(8,128)(2,1)}) custom-call(s32[32]{0:T(128)} %fusion.19.offset_ref, bf16[416,512]{1,0:T(8,128)(2,1)} %bitcast.76, bf16[64,2176]{1,0:T(8,128)(2,1)} %copy-done.2, bf16[64,2176]{1,0:T(8,128)(2,1)} %copy-done.6, ...), custom_call_target="tpu_custom_call" | custom-call | tf_op jit(solution)/shard_map/pallas_call | solution.py:597
  58.5 7.0 %collective-permute-start.15 = (bf16[416,512]{1,0:T(8,128)(2,1)}, bf16[416,512]{1,0:T(8,128)(2,1)S(1)}, u32[]{:S(2)}, u32[]{:S(2)}) collective-permute-start(bf16[416,512]{1,0:T(8,128)(2,1)} %get-tuple-element.52.refs_0_.a_two_ref), channel_id=1, source_target_pairs={{0,1},{1,2},{2,3},{3,0},{4,5},{5,6},{6,7},{7,4},{8,9},{9,10},{10,1... | collective-permute-start | bytes 1277960 | tf_op jit(solution)/shard_map/ppermute | solution.py:447
  69.3 6.2 %shard_map.213 = (s32[8,1664]{1,0:T(8,128)}, s32[1664,128]{1,0:T(8,128)}) custom-call(s32[1,1664]{1,0:T(1,128)} %slice.145.order_row, s32[1664,1]{1,0:T(8,128)} %copy.88.order_col, s32[2,1664]{1,0:T(2,128)} %slice.147.routes_row, s32[1664,2]{1,0:T(8,128)} %copy.89.routes_col), custom_call_target="tpu_custom_call" | custom-call | tf_op jit(solution)/shard_map/pallas_call | solution.py:589
  78.5 11.3 %shard_map.214.cot_ref = bf16[8,496,512]{2,1,0:T(8,128)(2,1)} custom-call(s32[8,1,1664]{2,1,0:T(1,128)} %reshape.75.slot_row_ref, bf16[416,512]{1,0:T(8,128)(2,1)} %bitcast.74, bf16[416,512]{1,0:T(8,128)(2,1)} %copy-done.13, bf16[416,512]{1,0:T(8,128)(2,1)} %copy-done.12, bf16[416,512]{1,0:T(8,128)(2,1)} %copy-done.11), custom_call_target="tpu_custom_call" | custom-call | tf_op jit(solution)/shard_map/pallas_call | solution.py:621
  89.8 4.8 %collective-permute-done.15.refs_1_ = bf16[416,512]{1,0:T(8,128)(2,1)S(1)} collective-permute-done((bf16[416,512]{1,0:T(8,128)(2,1)}, bf16[416,512]{1,0:T(8,128)(2,1)S(1)}, u32[]{:S(2)}, u32[]{:S(2)}) %collective-permute-start.15) | collective-permute-done | bytes 426016 | tf_op jit(solution)/shard_map/ppermute | solution.py:447
  95.4 10.1 %shard_map.215 = (bf16[8,496,512]{2,1,0:T(8,128)(2,1)}, f32[8,1280]{1,0:T(8,128)}) custom-call(s32[8,1,1664]{2,1,0:T(1,128)} %reshape.75.slot_row_ref, bf16[512,2176]{1,0:T(8,128)(2,1)} %get-tuple-element.51.side_ref.pack_ref, bf16[416,512]{1,0:T(8,128)(2,1)} %get-tuple-element.52.refs_0_.a_two_ref, bf16[416,512]{1,0:T(8,128)(2,1)} %copy-done.16, ...), custom_call_target="tpu_custom_call" | custom-call | tf_op jit(solution)/shard_map/pallas_call | solution.py:635
  106.2 22.4 %shard_map.216 = (bf16[8,496,512]{2,1,0:T(8,128)(2,1)}, bf16[8,496,512]{2,1,0:T(8,128)(2,1)}, bf16[8,496,512]{2,1,0:T(8,128)(2,1)}, bf16[8,496,512]{2,1,0:T(8,128)(2,1)}, f32[8,1664]{1,0:T(8,128)}) custom-call(s32[8,1,1664]{2,1,0:T(1,128)} %reshape.75.slot_row_ref, bf16[8,496,512]{2,1,0:T(8,128)(2,1)} %shard_map.214.cot_ref, ...), custom_call_target="tpu_custom_call" | custom-call | tf_op jit(solution)/shard_map/pallas_call | solution.py:647
  128.6 13.0 %shard_map.222 = bf16[8,2,512,512]{3,2,1,0:T(8,128)(2,1)} custom-call(bf16[8,496,512]{2,1,0:T(8,128)(2,1)} %get-tuple-element.77.rows_ref, bf16[8,496,512]{2,1,0:T(8,128)(2,1)} %shard_map.214.cot_ref, bf16[8,496,512]{2,1,0:T(8,128)(2,1)} %get-tuple-element.55.weighted_ref, bf16[8,496,512]{2,1,0:T(8,128)(2,1)} %get-tuple-element.78.grad_pre_ref), custom_call_target="tpu_custom_call" | custom-call | tf_op jit(solution)/shard_map/pallas_call | solution.py:688
  141.7 7.8 %shard_map.220 = bf16[432,512]{1,0:T(8,128)(2,1)} custom-call(s32[1664,128]{1,0:T(8,128)} %get-tuple-element.47.slot_col_ref, bf16[8,496,512]{2,1,0:T(8,128)(2,1)} %get-tuple-element.60.grad_in_ref, f32[8,1664]{1,0:T(8,128)} %get-tuple-element.61.grad_gates_ref), custom_call_target="tpu_custom_call" | custom-call | tf_op jit(solution)/shard_map/pallas_call | solution.py:675
  149.4 9.2 %shard_map.219 = (bf16[432,512]{1,0:T(8,128)(2,1)}, bf16[432,512]{1,0:T(8,128)(2,1)}) custom-call(s32[1664,128]{1,0:T(8,128)} %get-tuple-element.47.slot_col_ref, bf16[8,496,512]{2,1,0:T(8,128)(2,1)} %get-tuple-element.60.grad_in_ref, f32[8,1664]{1,0:T(8,128)} %get-tuple-element.61.grad_gates_ref), custom_call_target="tpu_custom_call" | custom-call | tf_op jit(solution)/shard_map/pallas_call | solution.py:675
  159.6 15.9 %collective-permute-start.19 = (bf16[432,512]{1,0:T(8,128)(2,1)}, bf16[432,512]{1,0:T(8,128)(2,1)S(1)}, u32[]{:S(2)}, u32[]{:S(2)}) collective-permute-start(bf16[432,512]{1,0:T(8,128)(2,1)} %get-tuple-element.63), channel_id=1, source_target_pairs={{0,1},{1,2},{2,3},{3,0},{4,5},{5,6},{6,7},{7,4},{8,9},{9,10},{10,1... | collective-permute-start | bytes 1327112 | tf_op jit(solution)/shard_map/ppermute | solution.py:447
  176.9 7.9 %shard_map.218.refs_0_ = bf16[432,512]{1,0:T(8,128)(2,1)} custom-call(s32[1664,128]{1,0:T(8,128)} %get-tuple-element.47.slot_col_ref, bf16[8,496,512]{2,1,0:T(8,128)(2,1)} %get-tuple-element.60.grad_in_ref, f32[8,1664]{1,0:T(8,128)} %get-tuple-element.61.grad_gates_ref), custom_call_target="tpu_custom_call" | custom-call | tf_op jit(solution)/shard_map/pallas_call | solution.py:675
  184.8 15.2 %shard_map.217 = (bf16[416,512]{1,0:T(8,128)(2,1)}, bf16[416,512]{1,0:T(8,128)(2,1)}, bf16[416,512]{1,0:T(8,128)(2,1)}, bf16[416,512]{1,0:T(8,128)(2,1)}) custom-call(s32[1664,128]{1,0:T(8,128)} %get-tuple-element.47.slot_col_ref, bf16[8,496,512]{2,1,0:T(8,128)(2,1)} %get-tuple-element.55.weighted_ref, ...), custom_call_target="tpu_custom_call" | custom-call | tf_op jit(solution)/shard_map/pallas_call | solution.py:697
  200.1 15.7 %collective-permute-done.20.refs_3_ = bf16[432,512]{1,0:T(8,128)(2,1)S(1)} collective-permute-done((bf16[432,512]{1,0:T(8,128)(2,1)S(1)}, bf16[432,512]{1,0:T(8,128)(2,1)S(1)}, u32[]{:S(2)}, u32[]{:S(2)}) %collective-permute-start.20) | collective-permute-done | bytes 442400 | tf_op jit(solution)/shard_map/ppermute | solution.py:447
  216.5 14.7 %shard_map.221 = (bf16[416,512]{1,0:T(8,128)(2,1)}, bf16[256,2176]{1,0:T(8,128)(2,1)}, bf16[256,2176]{1,0:T(8,128)(2,1)}) custom-call(s32[32]{0:T(128)} %fusion.19.offset_ref, bf16[416,512]{1,0:T(8,128)(2,1)} %get-tuple-element.52.refs_0_.a_two_ref, f32[416,512]{1,0:T(8,128)} %get-tuple-element.46.y_ref, bf16[416,512]{1,0:T(8,128)(2,1)} %bitcast.75, ...), custom_call_target="tpu_custom_call" | custom-call | tf_op jit(solution)/shard_map/pallas_call | solution.py:709
  231.2 3.0 collective-permute-done.24
  237.4 4.1 %collective-permute-done.27 = bf16[2,16,2176]{2,1,0:T(8,128)(2,1)S(1)} collective-permute-done((bf16[2,16,2176]{2,1,0:T(8,128)(2,1)S(1)}, bf16[2,16,2176]{2,1,0:T(8,128)(2,1)S(1)}, u32[]{:S(2)}, u32[]{:S(2)}) %collective-permute-start.27) | collective-permute-done | bytes 139296 | tf_op jit(solution)/shard_map/ppermute | solution.py:452
  252.6 15.0 %collective-permute-done.21 = bf16[416,512]{1,0:T(8,128)(2,1)S(1)} collective-permute-done((bf16[416,512]{1,0:T(8,128)(2,1)}, bf16[416,512]{1,0:T(8,128)(2,1)S(1)}, u32[]{:S(2)}, u32[]{:S(2)}) %collective-permute-start.21) | collective-permute-done | bytes 426016 | tf_op jit(solution)/shard_map/ppermute | solution.py:447
  267.6 8.6 %collective-permute-start.30 = (bf16[16,2176]{1,0:T(8,128)(2,1)S(1)}, bf16[16,2176]{1,0:T(8,128)(2,1)S(1)}, u32[]{:S(2)}, u32[]{:S(2)}) collective-permute-start(bf16[16,2176]{1,0:T(8,128)(2,1)S(1)} %get-tuple-element.148), channel_id=1, source_target_pairs={{0,1},{1,2},{2,3},{3,0},{4,5},{5,6},{6,7},{7,4},{8,9},{9,10},{10,1... | collective-permute-start | bytes 208904 | tf_op jit(solution)/shard_map/ppermute | solution.py:447
  276.3 9.3 %collective-permute-done.23 = bf16[416,512]{1,0:T(8,128)(2,1)S(1)} collective-permute-done((bf16[416,512]{1,0:T(8,128)(2,1)}, bf16[416,512]{1,0:T(8,128)(2,1)S(1)}, u32[]{:S(2)}, u32[]{:S(2)}) %collective-permute-start.23) | collective-permute-done | bytes 426016 | tf_op jit(solution)/shard_map/ppermute | solution.py:447
  (172 shorter events, 58.9 us)
Async XLA Ops:
  7.2 98.3 %all-gather.2.cloned.1.call-start = ((), (), s32[]{:S(2)}) async-start(), calls=%async_computation.1 | async-start | bytes 9437184 | tf_op jit(solution)/shard_map/all_gather | solution.py:576
  12.9 8.6 %collective-permute-start.2 = (bf16[16,2176]{1,0:T(8,128)(2,1)S(1)}, bf16[16,2176]{1,0:T(8,128)(2,1)S(1)}, u32[]{:S(2)}, u32[]{:S(2)}) collective-permute-start(bf16[16,2176]{1,0:T(8,128)(2,1)S(1)} %pad.17), channel_id=1, source_target_pairs={{0,3},{1,0},{2,1},{3,2},{4,7},{5,4},{6,5},{7,6},{8,11},{9,8},{10,9... | collective-permute-start | bytes 208904 | tf_op jit(solution)/shard_map/ppermute | solution.py:447
  24.9 264.9 %reduce-scatter.2.cloned.1.call-start = ((), (), s32[]{:S(2)}) async-start(), calls=%async_computation.2 | async-start | bytes 9437184 | tf_op jit(solution)/shard_map/reduce_scatter | solution.py:695
  25.0 8.6 %collective-permute-start.4 = (bf16[64,2176]{1,0:T(8,128)(2,1)S(1)}, bf16[64,2176]{1,0:T(8,128)(2,1)S(1)}, u32[]{:S(2)}, u32[]{:S(2)}) collective-permute-start(bf16[64,2176]{1,0:T(8,128)(2,1)S(1)} %pad_maximum_fusion.1.refs_0_), channel_id=1, source_target_pairs={{0,16},{16,0},{1,17},{17,1},{2,18},{18,2},{3,19},{19,3},{4,20},{20... | collective-permute-start | bytes 835592 | tf_op jit(solution)/shard_map/ppermute | solution.py:452
  26.6 9.4 %collective-permute-start.3 = (bf16[64,2176]{1,0:T(8,128)(2,1)S(1)}, bf16[64,2176]{1,0:T(8,128)(2,1)S(1)}, u32[]{:S(2)}, u32[]{:S(2)}) collective-permute-start(bf16[64,2176]{1,0:T(8,128)(2,1)S(1)} %pad_maximum_fusion.1.refs_0_), channel_id=1, source_target_pairs={{0,8},{4,12},{8,0},{12,4},{1,9},{5,13},{9,1},{13,5},{2,10},{6,14},... | collective-permute-start | bytes 835592 | tf_op jit(solution)/shard_map/ppermute | solution.py:452
  28.0 10.4 %collective-permute-start.7 = (bf16[64,2176]{1,0:T(8,128)(2,1)S(1)}, bf16[64,2176]{1,0:T(8,128)(2,1)S(1)}, u32[]{:S(2)}, u32[]{:S(2)}) collective-permute-start(bf16[64,2176]{1,0:T(8,128)(2,1)S(1)} %pad_maximum_fusion.1.refs_0_), channel_id=1, source_target_pairs={{0,4},{4,0},{8,12},{12,8},{1,5},{5,1},{9,13},{13,9},{2,6},{6,2},{1... | collective-permute-start | bytes 835592 | tf_op jit(solution)/shard_map/ppermute | solution.py:452
  33.6 8.9 %collective-permute-start.5 = (bf16[32,2176]{1,0:T(8,128)(2,1)S(1)}, bf16[32,2176]{1,0:T(8,128)(2,1)S(1)}, u32[]{:S(2)}, u32[]{:S(2)}) collective-permute-start(bf16[32,2176]{1,0:T(8,128)(2,1)S(1)} %slice.139), channel_id=1, source_target_pairs={{0,8},{4,12},{8,0},{12,4},{1,9},{5,13},{9,1},{13,5},{2,10},{6,14},... | collective-permute-start | bytes 417800 | tf_op jit(solution)/shard_map/ppermute | solution.py:452
  36.0 8.7 %collective-permute-start.6 = (bf16[32,2176]{1,0:T(8,128)(2,1)S(1)}, bf16[32,2176]{1,0:T(8,128)(2,1)}, u32[]{:S(2)}, u32[]{:S(2)}) collective-permute-start(bf16[32,2176]{1,0:T(8,128)(2,1)S(1)} %slice.140), channel_id=1, source_target_pairs={{0,16},{16,0},{1,17},{17,1},{2,18},{18,2},{3,19},{19,3},{4,20},{20... | collective-permute-start | bytes 417800 | tf_op jit(solution)/shard_map/ppermute | solution.py:452
  37.0 21.5 %collective-permute-start.14 = (bf16[416,512]{1,0:T(8,128)(2,1)S(1)}, bf16[416,512]{1,0:T(8,128)(2,1)S(1)}, u32[]{:S(2)}, u32[]{:S(2)}) collective-permute-start(bf16[416,512]{1,0:T(8,128)(2,1)S(1)} %bitcast.71), channel_id=1, source_target_pairs={{0,2},{1,3},{2,0},{3,1},{4,6},{5,7},{6,4},{7,5},{8,10},{9,11},{10,... | collective-permute-start | bytes 1277960 | tf_op jit(solution)/shard_map/ppermute | solution.py:447
  38.5 9.8 %collective-permute-start.8 = (bf16[64,2176]{1,0:T(8,128)(2,1)S(1)}, bf16[64,2176]{1,0:T(8,128)(2,1)}, u32[]{:S(2)}, u32[]{:S(2)}) collective-permute-start(bf16[64,2176]{1,0:T(8,128)(2,1)S(1)} %collective-permute-done.3.refs_1_), channel_id=1, source_target_pairs={{0,4},{4,0},{8,12},{12,8},{1,5},{5,1},{9,13},{13,9},{2,6},{6,2},{1... | collective-permute-start | bytes 835592 | tf_op jit(solution)/shard_map/ppermute | solution.py:452
  46.1 30.9 %collective-permute-start.13 = (bf16[416,512]{1,0:T(8,128)(2,1)S(1)}, bf16[416,512]{1,0:T(8,128)(2,1)S(1)}, u32[]{:S(2)}, u32[]{:S(2)}) collective-permute-start(bf16[416,512]{1,0:T(8,128)(2,1)S(1)} %bitcast.72), channel_id=1, source_target_pairs={{0,3},{1,0},{2,1},{3,2},{4,7},{5,4},{6,5},{7,6},{8,11},{9,8},{10,9... | collective-permute-start | bytes 1277960 | tf_op jit(solution)/shard_map/ppermute | solution.py:447
  46.8 30.2 %collective-permute-start.12 = (bf16[416,512]{1,0:T(8,128)(2,1)S(1)}, bf16[416,512]{1,0:T(8,128)(2,1)S(1)}, u32[]{:S(2)}, u32[]{:S(2)}) collective-permute-start(bf16[416,512]{1,0:T(8,128)(2,1)S(1)} %bitcast.73), channel_id=1, source_target_pairs={{0,1},{1,2},{2,3},{3,0},{4,5},{5,6},{6,7},{7,4},{8,9},{9,10},{10,1... | collective-permute-start | bytes 1277960 | tf_op jit(solution)/shard_map/ppermute | solution.py:447
  56.1 49.3 %collective-permute-start.17 = (bf16[416,512]{1,0:T(8,128)(2,1)}, bf16[416,512]{1,0:T(8,128)(2,1)S(1)}, u32[]{:S(2)}, u32[]{:S(2)}) collective-permute-start(bf16[416,512]{1,0:T(8,128)(2,1)} %get-tuple-element.52.refs_0_.a_two_ref), channel_id=1, source_target_pairs={{0,2},{1,3},{2,0},{3,1},{4,6},{5,7},{6,4},{7,5},{8,10},{9,11},{10,... | collective-permute-start | bytes 1277960 | tf_op jit(solution)/shard_map/ppermute | solution.py:447
  56.2 33.7 %collective-permute-start.16 = (bf16[416,512]{1,0:T(8,128)(2,1)}, bf16[416,512]{1,0:T(8,128)(2,1)S(1)}, u32[]{:S(2)}, u32[]{:S(2)}) collective-permute-start(bf16[416,512]{1,0:T(8,128)(2,1)} %get-tuple-element.52.refs_0_.a_two_ref), channel_id=1, source_target_pairs={{0,3},{1,0},{2,1},{3,2},{4,7},{5,4},{6,5},{7,6},{8,11},{9,8},{10,9... | collective-permute-start | bytes 1277960 | tf_op jit(solution)/shard_map/ppermute | solution.py:447
  58.5 36.1 %collective-permute-start.15 = (bf16[416,512]{1,0:T(8,128)(2,1)}, bf16[416,512]{1,0:T(8,128)(2,1)S(1)}, u32[]{:S(2)}, u32[]{:S(2)}) collective-permute-start(bf16[416,512]{1,0:T(8,128)(2,1)} %get-tuple-element.52.refs_0_.a_two_ref), channel_id=1, source_target_pairs={{0,1},{1,2},{2,3},{3,0},{4,5},{5,6},{6,7},{7,4},{8,9},{9,10},{10,1... | collective-permute-start | bytes 1277960 | tf_op jit(solution)/shard_map/ppermute | solution.py:447
  158.6 41.4 %collective-permute-start.18 = (bf16[432,512]{1,0:T(8,128)(2,1)}, bf16[432,512]{1,0:T(8,128)(2,1)S(1)}, u32[]{:S(2)}, u32[]{:S(2)}) collective-permute-start(bf16[432,512]{1,0:T(8,128)(2,1)} %get-tuple-element.62), channel_id=1, source_target_pairs={{0,3},{1,0},{2,1},{3,2},{4,7},{5,4},{6,5},{7,6},{8,11},{9,8},{10,9... | collective-permute-start | bytes 1327112 | tf_op jit(solution)/shard_map/ppermute | solution.py:447
  159.6 40.4 %collective-permute-start.19 = (bf16[432,512]{1,0:T(8,128)(2,1)}, bf16[432,512]{1,0:T(8,128)(2,1)S(1)}, u32[]{:S(2)}, u32[]{:S(2)}) collective-permute-start(bf16[432,512]{1,0:T(8,128)(2,1)} %get-tuple-element.63), channel_id=1, source_target_pairs={{0,1},{1,2},{2,3},{3,0},{4,5},{5,6},{6,7},{7,4},{8,9},{9,10},{10,1... | collective-permute-start | bytes 1327112 | tf_op jit(solution)/shard_map/ppermute | solution.py:447
  175.5 40.3 %collective-permute-start.20 = (bf16[432,512]{1,0:T(8,128)(2,1)S(1)}, bf16[432,512]{1,0:T(8,128)(2,1)S(1)}, u32[]{:S(2)}, u32[]{:S(2)}) collective-permute-start(bf16[432,512]{1,0:T(8,128)(2,1)S(1)} %copy-done.7), channel_id=1, source_target_pairs={{0,2},{1,3},{2,0},{3,1},{4,6},{5,7},{6,4},{7,5},{8,10},{9,11},{10,... | collective-permute-start | bytes 1327112 | tf_op jit(solution)/shard_map/ppermute | solution.py:447
  245.6 22.0 %collective-permute-start.21 = (bf16[416,512]{1,0:T(8,128)(2,1)}, bf16[416,512]{1,0:T(8,128)(2,1)S(1)}, u32[]{:S(2)}, u32[]{:S(2)}) collective-permute-start(bf16[416,512]{1,0:T(8,128)(2,1)} %get-tuple-element.65), channel_id=1, source_target_pairs={{0,3},{1,0},{2,1},{3,2},{4,7},{5,4},{6,5},{7,6},{8,11},{9,8},{10,9... | collective-permute-start | bytes 1277960 | tf_op jit(solution)/shard_map/ppermute | solution.py:447
  245.6 30.6 %collective-permute-start.22 = (bf16[416,512]{1,0:T(8,128)(2,1)}, bf16[416,512]{1,0:T(8,128)(2,1)S(1)}, u32[]{:S(2)}, u32[]{:S(2)}) collective-permute-start(bf16[416,512]{1,0:T(8,128)(2,1)} %get-tuple-element.66), channel_id=1, source_target_pairs={{0,1},{1,2},{2,3},{3,0},{4,5},{5,6},{6,7},{7,4},{8,9},{9,10},{10,1... | collective-permute-start | bytes 1277960 | tf_op jit(solution)/shard_map/ppermute | solution.py:447
  247.7 37.9 %collective-permute-start.23 = (bf16[416,512]{1,0:T(8,128)(2,1)}, bf16[416,512]{1,0:T(8,128)(2,1)S(1)}, u32[]{:S(2)}, u32[]{:S(2)}) collective-permute-start(bf16[416,512]{1,0:T(8,128)(2,1)} %get-tuple-element.67), channel_id=1, source_target_pairs={{0,2},{1,3},{2,0},{3,1},{4,6},{5,7},{6,4},{7,5},{8,10},{9,11},{10,... | collective-permute-start | bytes 1277960 | tf_op jit(solution)/shard_map/ppermute | solution.py:447
  252.5 34.3 %collective-permute-start.29 = (bf16[16,2176]{1,0:T(8,128)(2,1)S(1)}, bf16[16,2176]{1,0:T(8,128)(2,1)S(1)}, u32[]{:S(2)}, u32[]{:S(2)}) collective-permute-start(bf16[16,2176]{1,0:T(8,128)(2,1)S(1)} %get-tuple-element.146), channel_id=1, source_target_pairs={{0,3},{1,0},{2,1},{3,2},{4,7},{5,4},{6,5},{7,6},{8,11},{9,8},{10,9... | collective-permute-start | bytes 208904 | tf_op jit(solution)/shard_map/ppermute | solution.py:447
  252.5 34.5 %collective-permute-start.31 = (bf16[16,2176]{1,0:T(8,128)(2,1)S(1)}, bf16[16,2176]{1,0:T(8,128)(2,1)S(1)}, u32[]{:S(2)}, u32[]{:S(2)}) collective-permute-start(bf16[16,2176]{1,0:T(8,128)(2,1)S(1)} %get-tuple-element.147), channel_id=1, source_target_pairs={{0,2},{1,3},{2,0},{3,1},{4,6},{5,7},{6,4},{7,5},{8,10},{9,11},{10,... | collective-permute-start | bytes 208904 | tf_op jit(solution)/shard_map/ppermute | solution.py:447
  267.6 19.4 %collective-permute-start.30 = (bf16[16,2176]{1,0:T(8,128)(2,1)S(1)}, bf16[16,2176]{1,0:T(8,128)(2,1)S(1)}, u32[]{:S(2)}, u32[]{:S(2)}) collective-permute-start(bf16[16,2176]{1,0:T(8,128)(2,1)S(1)} %get-tuple-element.148), channel_id=1, source_target_pairs={{0,1},{1,2},{2,3},{3,0},{4,5},{5,6},{6,7},{7,4},{8,9},{9,10},{10,1... | collective-permute-start | bytes 208904 | tf_op jit(solution)/shard_map/ppermute | solution.py:447
  (36 other events, 397.8 us)
Sparse Core Ops, SparseCore 0:
  25.0 55.2 all-gather.1
  141.8 84.0 reduce-scatter.1
